TPU v7x, 128 devices: a whole 4x4x4 slice. The times are simulated.
128 devices in a mesh: dp: 8 (over x_hi, y), expert: 16 (over z, x_lo, core).
Axes of the slice: x: 4 (x_hi: 2, x_lo: 2; x = x_hi * 2 + x_lo), y: 4, z: 4, core: 2. Of those that a mesh axis runs over, the one named last changes fastest.
Arguments:
- tokens: bfloat16 [32768, 5120], P(('dp', 'expert')), may hold values from -6 to 6
- cotangent: bfloat16 [32768, 5120], P(('dp', 'expert')), may hold values from -6 to 6
- slot_token: int32 [128, 16, 8], P(('dp', 'expert')), may hold values from 0 to 255, as said below
- slot_weight: float32 [128, 16, 8], P(('dp', 'expert')), may hold values from 0.1 to 1
- w_gate: bfloat16 [16, 5120, 1536], P('expert', None, 'dp'), may hold values from -0.078125 to 0.078125
- w_up: bfloat16 [16, 5120, 1536], P('expert', None, 'dp'), may hold values from -0.078125 to 0.078125
- w_down: bfloat16 [16, 1536, 5120], P('expert', 'dp'), may hold values from -0.15625 to 0.15625
Outputs:
- moe_out: bfloat16 [32768, 5120], P(('dp', 'expert'))
- grad_tokens: bfloat16 [32768, 5120], P(('dp', 'expert'))
- grad_gate: bfloat16 [16, 5120, 1536], P('expert', None, 'dp')
- grad_up: bfloat16 [16, 5120, 1536], P('expert', None, 'dp')
- grad_down: bfloat16 [16, 1536, 5120], P('expert', 'dp')
Inputs may be any that keep to these rules, and one draw needn't show every extreme that they name: `slot_token`: each of the 128 x 16 rows of 8 entries names distinct tokens of its source device.
All inputs are finite; a program needn't handle non-finite values.
Results may differ from a plain program's by a relative error of at most 0.017.
Values may be sent and summed in bfloat16 or wider, within the bound.
A program may use at most 192 MiB of HBM per device.

v0:
```python
import jax
import jax.numpy as jnp
from jax import lax
from jax.sharding import PartitionSpec as P


def silu_parts(pre_gate):
    sigma_value = jax.nn.sigmoid(pre_gate)
    return (pre_gate * sigma_value, sigma_value * (1.0 + pre_gate * (1.0 - sigma_value)))


def combine(chosen, scales, arrived, token_count):
    table_rows = (chosen[None, :] == jnp.arange(token_count, dtype=jnp.int32)[:, None]).astype(
        jnp.float32
    ) * scales[None, :]
    return jnp.dot(table_rows, arrived.astype(jnp.float32), precision=lax.Precision.HIGHEST)


def dispatch(sent_tokens, sent_grads):
    landed = (
        lax.all_to_all(sent_tokens, "expert", split_axis=0, concat_axis=0, tiled=True),
        lax.all_to_all(sent_grads, "expert", split_axis=0, concat_axis=0, tiled=True),
    )
    shared = (
        lax.all_gather(landed[0], "dp", axis=0, tiled=True),
        lax.all_gather(landed[1], "dp", axis=0, tiled=True),
    )
    return (shared[0], shared[1])


def collect(term_of, own_rows):
    summed = lax.psum_scatter(
        term_of(jnp.int32(0), own_rows * lax.axis_size("dp")).astype(jnp.bfloat16),
        "dp",
        scatter_dimension=0,
        tiled=True,
    )
    return lax.all_to_all(summed, "expert", split_axis=0, concat_axis=0, tiled=True)


def on_device(tokens, cotangent, slot_token, slot_weight, w_gate, w_up, w_down):
    token_count = tokens.shape[0]
    chosen = slot_token.reshape(-1)
    scales = slot_weight.reshape(-1)
    own_rows = chosen.shape[0]
    sent_tokens = jnp.take(tokens, chosen, axis=0)
    sent_grads = (jnp.take(cotangent, chosen, axis=0).astype(jnp.float32) * scales[:, None]).astype(
        jnp.bfloat16
    )
    token_rows, grad_rows = dispatch(sent_tokens, sent_grads)
    local_gate = w_gate[0]
    local_up = w_up[0]
    local_down = w_down[0]
    gate_value = jnp.dot(token_rows, local_gate, preferred_element_type=jnp.float32)
    upward = jnp.dot(token_rows, local_up, preferred_element_type=jnp.float32)
    active, slope_term = silu_parts(gate_value)
    hidden = (active * upward).astype(jnp.bfloat16)

    def down_term(offset, length):
        return jnp.dot(hidden, local_down, preferred_element_type=jnp.float32)

    returned = collect(down_term, own_rows)
    moe_out = combine(chosen, scales, returned, token_count).astype(jnp.bfloat16)
    hidden_grad = jnp.einsum("rd,fd->rf", grad_rows, local_down, preferred_element_type=jnp.float32)
    gate_grad = (hidden_grad * upward * slope_term).astype(jnp.bfloat16)
    upward_grad = (hidden_grad * active).astype(jnp.bfloat16)
    grad_down = jnp.einsum(
        "rf,rd->fd", hidden, grad_rows, preferred_element_type=jnp.float32
    ).astype(jnp.bfloat16)
    grad_gate = jnp.einsum(
        "rd,rf->df", token_rows, gate_grad, preferred_element_type=jnp.float32
    ).astype(jnp.bfloat16)
    grad_up = jnp.einsum(
        "rd,rf->df", token_rows, upward_grad, preferred_element_type=jnp.float32
    ).astype(jnp.bfloat16)

    def input_term(offset, length):
        first_term = jnp.einsum(
            "rf,df->rd", gate_grad, local_gate, preferred_element_type=jnp.float32
        )
        second_term = jnp.einsum(
            "rf,df->rd", upward_grad, local_up, preferred_element_type=jnp.float32
        )
        return first_term + second_term

    returned_grad = collect(input_term, own_rows)
    grad_tokens = combine(chosen, jnp.ones_like(scales), returned_grad, token_count).astype(
        jnp.bfloat16
    )
    return (moe_out, grad_tokens, grad_gate[None], grad_up[None], grad_down[None])


def solution(mesh):
    in_specs = (
        P(("dp", "expert"), None),
        P(("dp", "expert"), None),
        P(("dp", "expert"), None, None),
        P(("dp", "expert"), None, None),
        P("expert", None, "dp"),
        P("expert", None, "dp"),
        P("expert", "dp", None),
    )
    out_specs = (
        P(("dp", "expert"), None),
        P(("dp", "expert"), None),
        P("expert", None, "dp"),
        P("expert", None, "dp"),
        P("expert", "dp", None),
    )
    return jax.shard_map(
        on_device, mesh=mesh, in_specs=in_specs, out_specs=out_specs, check_vma=False
    )
```

profile of v0, /device:TPU:1, one launch (start us, length us, event | category | flops | bytes accessed | tf_op | source)
XLA Modules:
  0.0 622.0 jit_solution(188519037601963671)
XLA Ops:
  7.2 0.0 copy-start
  7.2 0.0 all-gather.3.cloned.1.call-start
  7.2 0.9 copy.14
  8.1 0.1 eq.8
  8.3 0.7 copy-done
  8.9 2.4 gather_fusion
  11.3 1.5 select_bitcast_fusion
  12.8 0.0 copy-start.6
  12.8 0.0 copy-start.2
  12.8 26.3 %all_to_all.48 = bf16[16,8,5120]{2,1,0:T(8,128)(2,1)} all-to-all(bf16[16,8,5120]{2,1,0:T(8,128)(2,1)S(1)} %select_bitcast_fusion), channel_id=1, replica_groups=mesh['dp'=8,'expert'=16] {'expert'}, dimensions={0} | all-to-all | bytes 2621440 | tf_op jit(solution)/shard_map/all_to_all | solution.py:21
  39.2 0.0 all-gather.3.cloned.1.call-update
  39.2 0.0 all-gather.5.cloned.1.call-start
  39.2 0.0 copy-done.6
  39.2 0.1 copy.15
  39.3 0.1 mul.39
  39.4 0.0 copy-done.2
  39.4 2.4 gather_fusion.1
  41.8 1.7 fusion.13
  43.5 34.1 %all_to_all.49 = bf16[16,8,5120]{2,1,0:T(8,128)(2,1)} all-to-all(bf16[16,8,5120]{2,1,0:T(8,128)(2,1)S(1)} %fusion.13), channel_id=1, replica_groups=mesh['dp'=8,'expert'=16] {'expert'}, dimensions={0} | all-to-all | bytes 2621440 | tf_op jit(solution)/shard_map/all_to_all | solution.py:22
  77.6 0.0 all-gather.5.cloned.1.call-update
  77.6 0.2 reduce-scatter.3.cloned.1.call-start
  77.9 98.0 %all-gather.3.cloned.1.call-done = bf16[1024,5120]{1,0:T(8,128)(2,1)} async-done(((bf16[128,5120]{1,0:T(8,128)(2,1)}), bf16[1024,5120]{1,0:T(8,128)(2,1)}) %all-gather.3.cloned.1.call-update) | async-done | bytes 10485776 | tf_op jit(solution)/shard_map/all_gather | solution.py:25
  175.8 0.0 copy-start.7
  175.8 9.1 %fusion.7 = f32[1024,192]{0,1:T(8,128)} fusion(bf16[1024,5120]{1,0:T(8,128)(2,1)} %all-gather.3.cloned.1.call-done, bf16[1,5120,192]{1,2,0:T(8,128)(2,1)} %param.14), kind=kOutput, calls=%fused_computation.17 | convolution fusion | flops 2013265920 | bytes 13238272 | tf_op jit(solution)/shard_map/dot_general | solution.py:55
  185.0 0.0 copy-done.7
  185.0 0.0 copy-start.4
  185.0 6.4 %fusion.11 = f32[1024,192]{0,1:T(8,128)} fusion(bf16[1024,5120]{1,0:T(8,128)(2,1)S(1)} %copy-done.7, bf16[1,5120,192]{1,2,0:T(8,128)(2,1)} %param.13), kind=kOutput, calls=%fused_computation.21 | convolution fusion | flops 2013265920 | bytes 13238272 | tf_op jit(solution)/shard_map/dot_general | solution.py:54
  191.3 110.1 %all-gather.5.cloned.1.call-done = bf16[1024,5120]{1,0:T(8,128)(2,1)} async-done(((bf16[128,5120]{1,0:T(8,128)(2,1)}), bf16[1024,5120]{1,0:T(8,128)(2,1)}) %all-gather.5.cloned.1.call-update) | async-done | bytes 10485776 | tf_op jit(solution)/shard_map/all_gather | solution.py:26
  301.4 0.0 copy-done.4
  301.4 8.1 %multiply_convert_fusion.1 = (bf16[1024,192]{0,1:T(8,128)(2,1)S(1)}, bf16[1024,192]{0,1:T(8,128)(2,1)S(1)}, bf16[1024,192]{0,1:T(8,128)(2,1)S(1)}) fusion(f32[1024,192]{0,1:T(8,128)} %fusion.11, f32[1024,192]{0,1:T(8,128)} %fusion.7, bf16[1024,5120]{1,0:T(8,128)(2,1)} %all-gather.5.cloned.1.call-done, bf16[1,192,5120]{2,1,0:T(8,128)(2,1)S(1)} %copy-done.4), kind=kOutput, calls=%fused_computation.27 | convolution fusion | flops 2016215040 | bytes 15204352 | tf_op jit(solution)/shard_map/rd,fd->rf/dot_general | solution.py:64
  309.5 5.6 convolution_convert_fusion
  315.2 0.0 reduce-scatter.3.cloned.1.call-update
  315.2 0.3 reduce-scatter.5.cloned.1.call-start
  315.5 0.0 copy-start.5
  315.5 10.8 %fusion.9 = f32[1024,5120]{1,0:T(8,128)} fusion(bf16[1024,192]{0,1:T(8,128)(2,1)S(1)} %get-tuple-element.7, bf16[1,5120,192]{1,2,0:T(8,128)(2,1)} %param.13), kind=kOutput, calls=%fused_computation.19 | convolution fusion | flops 2013265920 | bytes 23330816 | tf_op jit(solution)/shard_map/rf,df->rd/dot_general | solution.py:78
  326.3 0.0 copy-done.5
  326.3 12.1 %add_convert_fusion = bf16[1024,5120]{1,0:T(8,128)(2,1)} fusion(f32[1024,5120]{1,0:T(8,128)} %fusion.9, bf16[1024,192]{0,1:T(8,128)(2,1)S(1)} %get-tuple-element.6, bf16[1,5120,192]{1,2,0:T(8,128)(2,1)S(1)} %copy-done.5), kind=kOutput, calls=%fused_computation.2 | convolution fusion | flops 2023751680 | bytes 33816576 | tf_op jit(solution)/shard_map/rf,df->rd/dot_general | solution.py:81
  338.4 0.0 reduce-scatter.5.cloned.1.call-update
  338.5 106.0 %reduce-scatter.3.cloned.1.call-done = bf16[128,5120]{1,0:T(8,128)(2,1)} async-done(((bf16[1024,5120]{1,0:T(8,128)(2,1)}), bf16[128,5120]{1,0:T(8,128)(2,1)}) %reduce-scatter.3.cloned.1.call-update) | async-done | bytes 1310736 | tf_op jit(solution)/shard_map/reduce_scatter | solution.py:32
  444.4 5.9 all-to-all-start.1
  450.3 7.5 %fusion = bf16[1,192,5120]{2,1,0:T(8,128)(2,1)} fusion(bf16[1024,192]{0,1:T(8,128)(2,1)S(1)} %get-tuple-element.8, bf16[1024,5120]{1,0:T(8,128)(2,1)} %all-gather.5.cloned.1.call-done), kind=kOutput, calls=%fused_computation.9 | convolution fusion | flops 2014248960 | bytes 12845056 | tf_op jit(solution)/shard_map/rf,rd->fd/dot_general | solution.py:67
  457.8 128.1 %reduce-scatter.5.cloned.1.call-done = bf16[128,5120]{1,0:T(8,128)(2,1)} async-done(((bf16[1024,5120]{1,0:T(8,128)(2,1)}), bf16[128,5120]{1,0:T(8,128)(2,1)}) %reduce-scatter.5.cloned.1.call-update) | async-done | bytes 1310736 | tf_op jit(solution)/shard_map/reduce_scatter | solution.py:32
  585.9 0.0 all-to-all-done.1
  585.9 0.0 copy-start.3
  585.9 5.9 all-to-all-start.3
  591.8 7.5 %fusion.2 = bf16[1,5120,192]{1,2,0:T(8,128)(2,1)} fusion(bf16[1024,192]{0,1:T(8,128)(2,1)S(1)} %get-tuple-element.6, bf16[1024,5120]{1,0:T(8,128)(2,1)} %all-gather.3.cloned.1.call-done), kind=kOutput, calls=%fused_computation.11 | convolution fusion | flops 2014248960 | bytes 12845056 | tf_op jit(solution)/shard_map/rd,rf->df/dot_general | solution.py:73
  599.2 0.0 copy-done.3
  599.2 7.5 %fusion.1 = bf16[1,5120,192]{1,2,0:T(8,128)(2,1)} fusion(bf16[1024,192]{0,1:T(8,128)(2,1)S(1)} %get-tuple-element.7, bf16[1024,5120]{1,0:T(8,128)(2,1)} %all-gather.3.cloned.1.call-done), kind=kOutput, calls=%fused_computation.10 | convolution fusion | flops 2014248960 | bytes 12845056 | tf_op jit(solution)/shard_map/rd,rf->df/dot_general | solution.py:70
  606.7 0.0 copy-start.1
  606.7 5.2 convolution_convert_fusion.2
  611.8 0.0 all-to-all-done.3
  611.8 3.6 convolution_convert_fusion.1
  615.5 0.0 copy-done.1
  (3 shorter events, 0.0 us)
Async XLA Ops:
  7.2 1.8 copy-start
  7.2 168.6 %all-gather.3.cloned.1.call-start = ((), (), s32[]{:S(2)}) async-start(), calls=%async_computation.6 | async-start | bytes 11796480 | tf_op jit(solution)/shard_map/all_gather | solution.py:25
  12.8 26.4 %copy-start.6 = (f32[1,16,8]{1,2,0:T(8,128)S(1)}, f32[1,16,8]{1,2,0:T(8,128)}, u32[]{:S(2)}) copy-start(f32[1,16,8]{1,2,0:T(8,128)} %param.12) | copy-start | bytes 1540
  12.8 26.6 %copy-start.2 = (bf16[256,5120]{1,0:T(8,128)(2,1)S(1)}, bf16[256,5120]{1,0:T(8,128)(2,1)}, u32[]{:S(2)}) copy-start(bf16[256,5120]{1,0:T(8,128)(2,1)} %param.10) | copy-start | bytes 7864324
  39.2 262.2 %all-gather.5.cloned.1.call-start = ((), (), s32[]{:S(2)}) async-start(), calls=%async_computation.8 | async-start | bytes 11796480 | tf_op jit(solution)/shard_map/all_gather | solution.py:26
  77.6 366.8 %reduce-scatter.3.cloned.1.call-start = ((), (), s32[]{:S(2)}) async-start(), calls=%async_computation.7 | async-start | bytes 11796480 | tf_op jit(solution)/shard_map/reduce_scatter | solution.py:32
  175.8 9.2 %copy-start.7 = (bf16[1024,5120]{1,0:T(8,128)(2,1)S(1)}, bf16[1024,5120]{1,0:T(8,128)(2,1)}, u32[]{:S(2)}) copy-start(bf16[1024,5120]{1,0:T(8,128)(2,1)} %all-gather.3.cloned.1.call-done) | copy-start | bytes 31457284
  185.0 116.5 %copy-start.4 = (bf16[1,192,5120]{2,1,0:T(8,128)(2,1)S(1)}, bf16[1,192,5120]{2,1,0:T(8,128)(2,1)}, u32[]{:S(2)}) copy-start(bf16[1,192,5120]{2,1,0:T(8,128)(2,1)} %param.15) | copy-start | bytes 5898244
  315.2 270.7 %reduce-scatter.5.cloned.1.call-start = ((), (), s32[]{:S(2)}) async-start(), calls=%async_computation.9 | async-start | bytes 11796480 | tf_op jit(solution)/shard_map/reduce_scatter | solution.py:32
  315.5 10.8 %copy-start.5 = (bf16[1,5120,192]{1,2,0:T(8,128)(2,1)S(1)}, bf16[1,5120,192]{1,2,0:T(8,128)(2,1)}, u32[]{:S(2)}) copy-start(bf16[1,5120,192]{1,2,0:T(8,128)(2,1)} %param.14) | copy-start | bytes 5898244
  444.4 141.5 %all-to-all-start.1 = ((bf16[16,8,5120]{2,1,0:T(8,128)(2,1)}), bf16[16,8,5120]{2,1,0:T(8,128)(2,1)S(1)}, u32[]{:S(2)}, u32[]{:S(2)}) async-start(bf16[16,8,5120]{2,1,0:T(8,128)(2,1)} %bitcast.52), calls=%async_computation.2 | async-start | bytes 2621440 | tf_op jit(solution)/shard_map/all_to_all | solution.py:38
  585.9 13.3 %copy-start.3 = (bf16[16,8,5120]{2,1,0:T(8,128)(2,1)}, bf16[16,8,5120]{2,1,0:T(8,128)(2,1)S(1)}, u32[]{:S(2)}) copy-start(bf16[16,8,5120]{2,1,0:T(8,128)(2,1)S(1)} %all-to-all-done.1) | copy-start | bytes 3932164
  585.9 25.9 %all-to-all-start.3 = ((bf16[16,8,5120]{2,1,0:T(8,128)(2,1)}), bf16[16,8,5120]{2,1,0:T(8,128)(2,1)}, u32[]{:S(2)}, u32[]{:S(2)}) async-start(bf16[16,8,5120]{2,1,0:T(8,128)(2,1)} %bitcast.51), calls=%async_computation.5 | async-start | bytes 2621440 | tf_op jit(solution)/shard_map/all_to_all | solution.py:38
  606.7 8.8 %copy-start.1 = (bf16[256,5120]{1,0:T(8,128)(2,1)S(1)}, bf16[256,5120]{1,0:T(8,128)(2,1)}, u32[]{:S(2)}) copy-start(bf16[256,5120]{1,0:T(8,128)(2,1)} %param.9) | copy-start | bytes 7864324
Sparse Core Ops, SparseCore 0:
  39.3 136.4 all-gather.2
  178.1 123.2 all-gather.4
  315.3 129.0 reduce-scatter.2
  448.1 137.7 reduce-scatter.4
where the time goes:
time: 623 us; the launch traced here: 622 us
  waiting for transfers between devices  442 us (71%)
  matrix products  83.4 us (13%)
  blocking collectives  60.4 us (10%)
  between operations  13.9 us (2%)
  starting transfers between devices  12.3 us (2%)
  local copies, waits for them, and re-layouts  6.59 us (1%)
    reduce_scatter x2, waiting for transfers between devices, collect(): lax.psum_scatter(term_of(jnp.int32(0), own_rows * lax.axis_size('dp')).as...  234 us
    all_gather x1, waiting for transfers between devices, dispatch(): lax.all_gather(landed[1], 'dp', axis=0, tiled=True)  110 us
    all_gather x1, waiting for transfers between devices, dispatch(): lax.all_gather(landed[0], 'dp', axis=0, tiled=True)  98 us
    all_to_all x1, blocking collectives, dispatch(): lax.all_to_all(sent_grads, 'expert', split_axis=0, concat_axis=0, tiled=T...  34.1 us
    all_to_all x1, blocking collectives, dispatch(): lax.all_to_all(sent_tokens, 'expert', split_axis=0, concat_axis=0, tiled=...  26.3 us
  transfers between devices with their start and end apart: 6, of which 4 were waited for; matrix products, arithmetic and copies ran while one was open for 11% of the time, Pallas kernels for 0%

commit v1 on v0

v1 whole, which is shorter than its diff:
```python
import jax
import jax.numpy as jnp
from jax import lax
from jax.sharding import PartitionSpec as P

AXES = ("dp", "expert")


def silu_parts(pre_gate):
    sigma_value = jax.nn.sigmoid(pre_gate)
    return (pre_gate * sigma_value, sigma_value * (1.0 + pre_gate * (1.0 - sigma_value)))


def combine(chosen, scales, arrived, token_count):
    table_rows = (chosen[None, :] == jnp.arange(token_count, dtype=jnp.int32)[:, None]).astype(
        jnp.float32
    ) * scales[None, :]
    return jnp.dot(table_rows, arrived.astype(jnp.float32), precision=lax.Precision.HIGHEST)


def plans(n_dp, n_expert):
    n_y = n_dp // 2
    across, rows, weights = [], [], []
    for d in range(n_dp):
        x_hi, y = d // n_y, d % n_y
        for e in range(n_expert):
            me = d * n_expert + e
            core = e % 2
            near = y ^ 1
            far = (((y + 1) ^ 1) - 1) % n_y
            weight_y, row_y = (near, far) if core == 0 else (far, near)
            across.append((me, ((1 - x_hi) * n_y + y) * n_expert + e))
            rows.append((me, (x_hi * n_y + row_y) * n_expert + e))
            weights.append((me, (x_hi * n_y + weight_y) * n_expert + e))
    return across, rows, weights


def exchange(value, plan):
    return lax.ppermute(value, AXES, plan)


def dot(left, right, contract):
    return lax.dot_general(
        left, right, (contract, ((), ())), preferred_element_type=jnp.float32
    )


NN = ((1,), (0,))
NT = ((1,), (1,))
TN = ((0,), (0,))


def on_device(tokens, cotangent, slot_token, slot_weight, w_gate, w_up, w_down):
    across, row_pairs, weight_pairs = plans(lax.axis_size("dp"), lax.axis_size("expert"))
    token_count = tokens.shape[0]
    chosen = slot_token.reshape(-1)
    scales = slot_weight.reshape(-1)
    gates = [w_gate[0], exchange(w_gate[0], weight_pairs)]
    ups = [w_up[0], exchange(w_up[0], weight_pairs)]
    downs = [w_down[0], exchange(w_down[0], weight_pairs)]
    sent_tokens = jnp.take(tokens, chosen, axis=0)
    sent_grads = (jnp.take(cotangent, chosen, axis=0).astype(jnp.float32) * scales[:, None]).astype(
        jnp.bfloat16
    )

    def spread(sent):
        landed = lax.all_to_all(sent, "expert", split_axis=0, concat_axis=0, tiled=True)
        two = jnp.concatenate([landed, exchange(landed, across)], axis=0)
        return [two, exchange(two, row_pairs)]

    def gather_back(parts):
        own, other = parts
        kept = own + exchange(other.astype(jnp.bfloat16), row_pairs).astype(jnp.float32)
        half = kept.shape[0] // 2
        away = exchange(kept[half:].astype(jnp.bfloat16), across)
        summed = (kept[:half] + away.astype(jnp.float32)).astype(jnp.bfloat16)
        return lax.all_to_all(summed, "expert", split_axis=0, concat_axis=0, tiled=True)

    token_rows = spread(sent_tokens)
    grad_rows = spread(sent_grads)
    token_all = jnp.concatenate(token_rows, axis=0)
    grad_all = jnp.concatenate(grad_rows, axis=0)
    half = token_all.shape[0] // 2
    hidden, gate_grad, upward_grad = [], [], []
    for s in range(2):
        gate_value = dot(token_all, gates[s], NN)
        upward = dot(token_all, ups[s], NN)
        active, slope_term = silu_parts(gate_value)
        hidden.append((active * upward).astype(jnp.bfloat16))
        hidden_grad = dot(grad_all, downs[s], NT)
        gate_grad.append((hidden_grad * upward * slope_term).astype(jnp.bfloat16))
        upward_grad.append((hidden_grad * active).astype(jnp.bfloat16))

    def out_part(rows):
        return dot(hidden[0][rows], downs[0], NN) + dot(hidden[1][rows], downs[1], NN)

    def input_part(rows):
        total = dot(gate_grad[0][rows], gates[0], NT) + dot(upward_grad[0][rows], ups[0], NT)
        return total + dot(gate_grad[1][rows], gates[1], NT) + dot(upward_grad[1][rows], ups[1], NT)

    first, second = slice(0, half), slice(half, 2 * half)
    returned = gather_back((out_part(first), out_part(second)))
    moe_out = combine(chosen, scales, returned, token_count).astype(jnp.bfloat16)
    returned_grad = gather_back((input_part(first), input_part(second)))
    grad_tokens = combine(chosen, jnp.ones_like(scales), returned_grad, token_count).astype(
        jnp.bfloat16
    )

    def weight_grad(of):
        away = exchange(of(1).astype(jnp.bfloat16), weight_pairs)
        return (of(0) + away.astype(jnp.float32)).astype(jnp.bfloat16)[None]

    grad_down = weight_grad(lambda s: dot(hidden[s], grad_all, TN))
    grad_gate = weight_grad(lambda s: dot(token_all, gate_grad[s], TN))
    grad_up = weight_grad(lambda s: dot(token_all, upward_grad[s], TN))
    return (moe_out, grad_tokens, grad_gate, grad_up, grad_down)


def solution(mesh):
    in_specs = (
        P(("dp", "expert"), None),
        P(("dp", "expert"), None),
        P(("dp", "expert"), None, None),
        P(("dp", "expert"), None, None),
        P("expert", None, "dp"),
        P("expert", None, "dp"),
        P("expert", "dp", None),
    )
    out_specs = (
        P(("dp", "expert"), None),
        P(("dp", "expert"), None),
        P("expert", None, "dp"),
        P("expert", None, "dp"),
        P("expert", "dp", None),
    )
    return jax.shard_map(
        on_device, mesh=mesh, in_specs=in_specs, out_specs=out_specs, check_vma=False
    )
```

time: 623 us -> 417 us (0.67)
  waiting for transfers between devices: 442 us -> 265 us
  blocking collectives: 60.4 us -> 0 us
  starting transfers between devices: 12.3 us -> 53.3 us
  matrix products: 83.4 us -> 69.2 us
  between operations: 13.9 us -> 0.96 us
  other arithmetic: 3.22 us -> 14 us
    reduce_scatter x2 -> x0, waiting for transfers between devices: 234 us -> none  [collect(): lax.psum_scatter(term_of(jnp.int32(0), own_rows * lax.axis_size('dp')).as...]
    ppermute x0 -> x14, waiting for transfers between devices: none -> 214 us  [exchange(): return lax.ppermute(value, AXES, plan)]
    all_gather x2 -> x0, waiting for transfers between devices: 208 us -> none  [the longest x1 110 us: dispatch(): lax.all_gather(landed[1], 'dp', axis=0, tiled=True)]
    all_to_all x2 -> x0, blocking collectives: 60.4 us -> none  [the longest x1 34.1 us: dispatch(): lax.all_to_all(sent_grads, 'expert', split_axis=0, concat_axis=0, tiled=T...]
    all_to_all x2 -> x4, waiting for transfers between devices: 0.01 us -> 51.4 us  [the longest x2 29.6 us: spread(): lax.all_to_all(sent, 'expert', split_axis=0, concat_axis=0, tiled=True)]
    all_to_all x2 -> x4, starting transfers between devices: 11.7 us -> 33.2 us  [the longest x2 20.4 us: gather_back(): lax.all_to_all(summed, 'expert', split_axis=0, concat_axis=0, tiled=True)]
    ppermute x0 -> x14, starting transfers between devices: none -> 20.1 us  [exchange(): return lax.ppermute(value, AXES, plan)]
    dot_general x9 -> x24, matrix products: 74.6 us -> 61.9 us  [dot(): lax.dot_general(left, right, (contract, ((), ())), preferred_element_type...]
  transfers between devices with their start and end apart: 6 -> 18, of which waited for: 4 -> 12; matrix products, arithmetic and copies ran while one was open for 11% -> 17% of each run, Pallas kernels for 0% -> 0%
where the time goes in v1:
time: 417 us; the launch traced here: 415 us
  waiting for transfers between devices  265 us (64%)
  matrix products  69.2 us (17%)
  starting transfers between devices  53.3 us (13%)
  other arithmetic  14 us (3%)
  local copies, waits for them, and re-layouts  11.9 us (3%)
    ppermute x14, waiting for transfers between devices, exchange(): return lax.ppermute(value, AXES, plan)  214 us
    dot_general x24, matrix products, dot(): lax.dot_general(left, right, (contract, ((), ())), preferred_element_type...  61.9 us
    all_to_all x2, waiting for transfers between devices, spread(): lax.all_to_all(sent, 'expert', split_axis=0, concat_axis=0, tiled=True)  29.6 us
    all_to_all x2, waiting for transfers between devices, gather_back(): lax.all_to_all(summed, 'expert', split_axis=0, concat_axis=0, tiled=True)  21.8 us
    all_to_all x2, starting transfers between devices, gather_back(): lax.all_to_all(summed, 'expert', split_axis=0, concat_axis=0, tiled=True)  20.4 us
    ppermute x14, starting transfers between devices, exchange(): return lax.ppermute(value, AXES, plan)  20.1 us
    all_to_all x2, starting transfers between devices, spread(): lax.all_to_all(sent, 'expert', split_axis=0, concat_axis=0, tiled=True)  12.8 us
  transfers between devices with their start and end apart: 18, of which 12 were waited for; matrix products, arithmetic and copies ran while one was open for 17% of the time, Pallas kernels for 0%

profile of v1, /device:TPU:1, one launch (start us, length us, event | category | flops | bytes accessed | tf_op | source)
XLA Modules:
  0.0 414.8 jit_solution(3847459882056378830)
XLA Ops:
  0.6 0.9 copy.14
  2.4 2.4 gather_fusion
  4.8 2.7 select_bitcast_fusion
  7.5 7.7 %all-to-all-start = ((bf16[16,8,5120]{2,1,0:T(8,128)(2,1)}), bf16[16,8,5120]{2,1,0:T(8,128)(2,1)}, u32[]{:S(2)}, u32[]{:S(2)}) async-start(bf16[16,8,5120]{2,1,0:T(8,128)(2,1)} %select_bitcast_fusion), calls=%async_computation | async-start | bytes 2621440 | tf_op jit(solution)/shard_map/all_to_all | solution.py:67
  15.4 2.4 gather_fusion.1
  17.8 2.8 fusion.14
  20.5 13.3 %all-to-all-done = bf16[16,8,5120]{2,1,0:T(8,128)(2,1)} async-done(((bf16[16,8,5120]{2,1,0:T(8,128)(2,1)}), bf16[16,8,5120]{2,1,0:T(8,128)(2,1)}, u32[]{:S(2)}, u32[]{:S(2)}) %all-to-all-start) | async-done | bytes 1310752 | tf_op jit(solution)/shard_map/all_to_all | solution.py:67
  33.8 5.1 %all-to-all-start.2 = ((bf16[16,8,5120]{2,1,0:T(8,128)(2,1)}), bf16[16,8,5120]{2,1,0:T(8,128)(2,1)}, u32[]{:S(2)}, u32[]{:S(2)}) async-start(bf16[16,8,5120]{2,1,0:T(8,128)(2,1)} %fusion.14), calls=%async_computation.2 | async-start | bytes 2621440 | tf_op jit(solution)/shard_map/all_to_all | solution.py:67
  38.9 2.5 collective-permute-start
  41.4 16.3 %all-to-all-done.2 = bf16[16,8,5120]{2,1,0:T(8,128)(2,1)} async-done(((bf16[16,8,5120]{2,1,0:T(8,128)(2,1)}), bf16[16,8,5120]{2,1,0:T(8,128)(2,1)}, u32[]{:S(2)}, u32[]{:S(2)}) %all-to-all-start.2) | async-done | bytes 1310752 | tf_op jit(solution)/shard_map/all_to_all | solution.py:67
  57.7 2.5 collective-permute-start.7
  60.1 25.3 %collective-permute-done = bf16[128,5120]{1,0:T(8,128)(2,1)S(1)} collective-permute-done((bf16[128,5120]{1,0:T(8,128)(2,1)}, bf16[128,5120]{1,0:T(8,128)(2,1)S(1)}, u32[]{:S(2)}, u32[]{:S(2)}) %collective-permute-start) | collective-permute-done | bytes 1310752 | tf_op jit(solution)/shard_map/ppermute | solution.py:39
  85.5 2.0 pad_maximum_fusion.2
  87.5 1.4 collective-permute-start.1
  88.9 24.7 %collective-permute-done.7 = bf16[128,5120]{1,0:T(8,128)(2,1)S(1)} collective-permute-done((bf16[128,5120]{1,0:T(8,128)(2,1)}, bf16[128,5120]{1,0:T(8,128)(2,1)S(1)}, u32[]{:S(2)}, u32[]{:S(2)}) %collective-permute-start.7) | collective-permute-done | bytes 1310752 | tf_op jit(solution)/shard_map/ppermute | solution.py:39
  113.5 2.0 pad_maximum_fusion.3
  115.5 1.4 collective-permute-start.8
  116.9 1.9 collective-permute-start.3
  118.8 0.8 collective-permute-start.4
  119.6 1.9 collective-permute-start.2
  121.5 41.5 %collective-permute-done.3 = bf16[5120,192]{0,1:T(8,128)(2,1)S(1)} collective-permute-done((bf16[5120,192]{0,1:T(8,128)(2,1)S(1)}, bf16[5120,192]{0,1:T(8,128)(2,1)S(1)}, u32[]{:S(2)}, u32[]{:S(2)}) %collective-permute-start.3) | collective-permute-done | bytes 1966112 | tf_op jit(solution)/shard_map/ppermute | solution.py:39
  162.9 4.1 fusion.58
  167.1 23.9 %collective-permute-done.4 = bf16[192,5120]{1,0:T(8,128)(2,1)S(1)} collective-permute-done((bf16[192,5120]{1,0:T(8,128)(2,1)S(1)}, bf16[192,5120]{1,0:T(8,128)(2,1)S(1)}, u32[]{:S(2)}, u32[]{:S(2)}) %collective-permute-start.4) | collective-permute-done | bytes 1966112 | tf_op jit(solution)/shard_map/ppermute | solution.py:39
  191.0 4.2 %fusion.57 = f32[512,192]{0,1:T(8,128)S(1)} fusion(bf16[192,5120]{1,0:T(8,128)(2,1)S(1)} %collective-permute-done.4, bf16[256,5120]{1,0:T(8,128)(2,1)S(1)} %collective-permute-done.8, bf16[128,5120]{1,0:T(8,128)(2,1)S(1)} %collective-permute-done.7, bf16[128,5120]{1,0:T(8,128)(2,1)} %bitcast.8), kind=kOutput, calls=%fused_computation.95 | convolution fusion | flops 1022361600 | bytes 7602176 | tf_op jit(solution)/shard_map/dot_general | solution.py:43
  195.2 16.8 %collective-permute-done.2 = bf16[5120,192]{0,1:T(8,128)(2,1)S(1)} collective-permute-done((bf16[5120,192]{0,1:T(8,128)(2,1)S(1)}, bf16[5120,192]{0,1:T(8,128)(2,1)S(1)}, u32[]{:S(2)}, u32[]{:S(2)}) %collective-permute-start.2) | collective-permute-done | bytes 1966112 | tf_op jit(solution)/shard_map/ppermute | solution.py:39
  212.0 3.4 multiply_convert_fusion.2
  215.4 3.9 convolution_convert_fusion.4
  219.3 2.7 collective-permute-start.13
  222.1 3.8 convolution_convert_fusion.2
  225.9 3.2 fusion.50
  229.1 3.2 fusion.54
  232.3 3.3 multiply_convert_fusion.3
  235.6 0.9 fusion.26
  236.5 0.9 convolution_add_fusion.1
  237.4 0.9 fusion.22
  238.3 2.4 fusion.5
  240.7 0.9 fusion.35
  241.6 0.9 fusion.4
  242.5 1.8 collective-permute-start.5
  244.3 0.9 fusion.32
  245.2 0.9 fusion.38
  246.1 0.9 convolution_add_fusion.3
  247.0 0.9 fusion.28
  247.9 43.1 %collective-permute-done.9 = bf16[256,5120]{1,0:T(8,128)(2,1)S(1)} collective-permute-done((bf16[256,5120]{1,0:T(8,128)(2,1)}, bf16[256,5120]{1,0:T(8,128)(2,1)S(1)}, u32[]{:S(2)}, u32[]{:S(2)}) %collective-permute-start.9) | collective-permute-done | bytes 2621472 | tf_op jit(solution)/shard_map/ppermute | solution.py:39
  290.9 1.1 fusion.3
  292.8 1.0 copy-done.20
  293.8 3.8 convolution_convert_fusion.3
  297.6 2.7 collective-permute-start.11
  300.4 34.2 %collective-permute-done.5 = bf16[256,5120]{1,0:T(8,128)(2,1)} collective-permute-done((bf16[256,5120]{1,0:T(8,128)(2,1)S(1)}, bf16[256,5120]{1,0:T(8,128)(2,1)}, u32[]{:S(2)}, u32[]{:S(2)}) %collective-permute-start.5) | collective-permute-done | bytes 2621472 | tf_op jit(solution)/shard_map/ppermute | solution.py:39
  334.5 2.9 fusion.2
  337.4 2.3 copy-done.3
  339.8 1.2 slice.123
  341.6 4.5 %fusion.11 = bf16[1,192,5120]{2,1,0:T(8,128)(2,1)} fusion(bf16[512,192]{0,1:T(8,128)(2,1)S(1)} %copy-done.15, bf16[192,5120]{1,0:T(8,128)(2,1)} %collective-permute-done.13, bf16[256,5120]{1,0:T(8,128)(2,1)S(1)} %copy-done.23, bf16[128,5120]{1,0:T(8,128)(2,1)S(1)} %copy-done.13, bf16[128,5120]{1,0:T(8,128)(2,1)} %bitcast.8), kind=kOutput, calls=%fused_computation.27 | convolution fusion | flops 1025310720 | bytes 9371648 | tf_op jit(solution)/shard_map/dot_general | solution.py:43
  346.0 1.4 fusion.16
  347.4 13.2 %all-to-all-start.3 = ((bf16[16,8,5120]{2,1,0:T(8,128)(2,1)}), bf16[16,8,5120]{2,1,0:T(8,128)(2,1)S(1)}, u32[]{:S(2)}, u32[]{:S(2)}) async-start(bf16[16,8,5120]{2,1,0:T(8,128)(2,1)} %fusion.16), calls=%async_computation.3 | async-start | bytes 2621440 | tf_op jit(solution)/shard_map/all_to_all | solution.py:77
  360.6 4.6 %collective-permute-done.6 = bf16[128,5120]{1,0:T(8,128)(2,1)S(1)} collective-permute-done((bf16[128,5120]{1,0:T(8,128)(2,1)}, bf16[128,5120]{1,0:T(8,128)(2,1)S(1)}, u32[]{:S(2)}, u32[]{:S(2)}) %collective-permute-start.6) | collective-permute-done | bytes 1310752 | tf_op jit(solution)/shard_map/ppermute | solution.py:39
  365.2 3.1 fusion.15
  368.4 15.5 %all-to-all-done.3 = bf16[16,8,5120]{2,1,0:T(8,128)(2,1)S(1)} async-done(((bf16[16,8,5120]{2,1,0:T(8,128)(2,1)}), bf16[16,8,5120]{2,1,0:T(8,128)(2,1)S(1)}, u32[]{:S(2)}, u32[]{:S(2)}) %all-to-all-start.3) | async-done | bytes 1310752 | tf_op jit(solution)/shard_map/all_to_all | solution.py:77
  383.9 7.2 %all-to-all-start.1 = ((bf16[16,8,5120]{2,1,0:T(8,128)(2,1)}), bf16[16,8,5120]{2,1,0:T(8,128)(2,1)}, u32[]{:S(2)}, u32[]{:S(2)}) async-start(bf16[16,8,5120]{2,1,0:T(8,128)(2,1)} %fusion.15), calls=%async_computation.1 | async-start | bytes 2621440 | tf_op jit(solution)/shard_map/all_to_all | solution.py:77
  391.1 5.4 %fusion.9 = bf16[1,5120,192]{1,2,0:T(8,128)(2,1)} fusion(bf16[512,192]{0,1:T(8,128)(2,1)S(1)} %get-tuple-element.9, bf16[5120,192]{0,1:T(8,128)(2,1)} %collective-permute-done.12, bf16[256,5120]{1,0:T(8,128)(2,1)} %copy-done.19, bf16[128,5120]{1,0:T(8,128)(2,1)S(1)} %copy-done.11, bf16[128,5120]{1,0:T(8,128)(2,1)} %bitcast.1), kind=kOutput, calls=%fused_computation.25 | convolution fusion | flops 1025310720 | bytes 9371648 | tf_op jit(solution)/shard_map/dot_general | solution.py:43
  396.6 4.6 %fusion.10 = bf16[1,5120,192]{1,2,0:T(8,128)(2,1)} fusion(bf16[512,192]{0,1:T(8,128)(2,1)S(1)} %get-tuple-element.10, bf16[5120,192]{0,1:T(8,128)(2,1)} %collective-permute-done.11, bf16[256,5120]{1,0:T(8,128)(2,1)S(1)} %copy-done.21, bf16[128,5120]{1,0:T(8,128)(2,1)S(1)} %copy-done.11, bf16[128,5120]{1,0:T(8,128)(2,1)} %bitcast.1), kind=kOutput, calls=%fused_computation.26 | convolution fusion | flops 1025310720 | bytes 9371648 | tf_op jit(solution)/shard_map/dot_general | solution.py:43
  401.2 2.3 convolution_convert_fusion
  403.5 6.3 %all-to-all-done.1 = bf16[16,8,5120]{2,1,0:T(8,128)(2,1)} async-done(((bf16[16,8,5120]{2,1,0:T(8,128)(2,1)}), bf16[16,8,5120]{2,1,0:T(8,128)(2,1)}, u32[]{:S(2)}, u32[]{:S(2)}) %all-to-all-start.1) | async-done | bytes 1310752 | tf_op jit(solution)/shard_map/all_to_all | solution.py:77
  409.8 5.0 %convolution_convert_fusion.1 = bf16[256,5120]{1,0:T(8,128)(2,1)} fusion(bf16[16,8,5120]{2,1,0:T(8,128)(2,1)} %all-to-all-done.1, f32[128]{0:T(128)S(1)} %mul.60, s32[128]{0:T(128)S(1)} %eq.8), kind=kOutput, calls=%fused_computation.16 | convolution fusion | flops 2014642176 | bytes 3933184 | tf_op jit(solution)/shard_map/dot_general | solution.py:18
  (63 shorter events, 2.4 us)
Async XLA Ops:
  0.6 1.8 copy-start
  4.8 10.5 %copy-start.18 = (f32[1,16,8]{1,2,0:T(8,128)S(1)}, f32[1,16,8]{1,2,0:T(8,128)}, u32[]{:S(2)}) copy-start(f32[1,16,8]{1,2,0:T(8,128)} %param.12) | copy-start | bytes 1540
  4.8 10.6 %copy-start.2 = (bf16[256,5120]{1,0:T(8,128)(2,1)S(1)}, bf16[256,5120]{1,0:T(8,128)(2,1)}, u32[]{:S(2)}) copy-start(bf16[256,5120]{1,0:T(8,128)(2,1)} %param.10) | copy-start | bytes 7864324
  7.5 26.4 %all-to-all-start = ((bf16[16,8,5120]{2,1,0:T(8,128)(2,1)}), bf16[16,8,5120]{2,1,0:T(8,128)(2,1)}, u32[]{:S(2)}, u32[]{:S(2)}) async-start(bf16[16,8,5120]{2,1,0:T(8,128)(2,1)} %select_bitcast_fusion), calls=%async_computation | async-start | bytes 2621440 | tf_op jit(solution)/shard_map/all_to_all | solution.py:67
  33.8 23.8 %all-to-all-start.2 = ((bf16[16,8,5120]{2,1,0:T(8,128)(2,1)}), bf16[16,8,5120]{2,1,0:T(8,128)(2,1)}, u32[]{:S(2)}, u32[]{:S(2)}) async-start(bf16[16,8,5120]{2,1,0:T(8,128)(2,1)} %fusion.14), calls=%async_computation.2 | async-start | bytes 2621440 | tf_op jit(solution)/shard_map/all_to_all | solution.py:67
  38.9 46.5 %collective-permute-start = (bf16[128,5120]{1,0:T(8,128)(2,1)}, bf16[128,5120]{1,0:T(8,128)(2,1)S(1)}, u32[]{:S(2)}, u32[]{:S(2)}) collective-permute-start(bf16[128,5120]{1,0:T(8,128)(2,1)} %bitcast.1), channel_id=1, source_target_pairs={{0,64},{1,65},{2,66},{3,67},{4,68},{5,69},{6,70},{7,71},{8,72},{9,... | collective-permute-start | bytes 3932168 | tf_op jit(solution)/shard_map/ppermute | solution.py:39
  57.7 55.9 %collective-permute-start.7 = (bf16[128,5120]{1,0:T(8,128)(2,1)}, bf16[128,5120]{1,0:T(8,128)(2,1)S(1)}, u32[]{:S(2)}, u32[]{:S(2)}) collective-permute-start(bf16[128,5120]{1,0:T(8,128)(2,1)} %bitcast.8), channel_id=1, source_target_pairs={{0,64},{1,65},{2,66},{3,67},{4,68},{5,69},{6,70},{7,71},{8,72},{9,... | collective-permute-start | bytes 3932168 | tf_op jit(solution)/shard_map/ppermute | solution.py:39
  85.4 2.0 copy-start.9
  85.5 31.4 %copy-start.6 = (bf16[1,5120,192]{1,2,0:T(8,128)(2,1)S(1)}, bf16[1,5120,192]{1,2,0:T(8,128)(2,1)}, u32[]{:S(2)}) copy-start(bf16[1,5120,192]{1,2,0:T(8,128)(2,1)} %param.14) | copy-start | bytes 5898244
  87.5 31.3 %copy-start.5 = (bf16[1,192,5120]{2,1,0:T(8,128)(2,1)S(1)}, bf16[1,192,5120]{2,1,0:T(8,128)(2,1)}, u32[]{:S(2)}) copy-start(bf16[1,192,5120]{2,1,0:T(8,128)(2,1)} %param.15) | copy-start | bytes 5898244
  87.5 32.1 %copy-start.4 = (bf16[1,5120,192]{1,2,0:T(8,128)(2,1)S(1)}, bf16[1,5120,192]{1,2,0:T(8,128)(2,1)}, u32[]{:S(2)}) copy-start(bf16[1,5120,192]{1,2,0:T(8,128)(2,1)} %param.13) | copy-start | bytes 5898244
  87.5 75.4 %collective-permute-start.1 = (bf16[256,5120]{1,0:T(8,128)(2,1)S(1)}, bf16[256,5120]{1,0:T(8,128)(2,1)S(1)}, u32[]{:S(2)}, u32[]{:S(2)}) collective-permute-start(bf16[256,5120]{1,0:T(8,128)(2,1)S(1)} %pad_maximum_fusion.2), channel_id=1, source_target_pairs={{0,48},{1,17},{2,50},{3,19},{4,52},{5,21},{6,54},{7,23},{8,56},{9,... | collective-permute-start | bytes 7864328 | tf_op jit(solution)/shard_map/ppermute | solution.py:39
  88.9 74.1 %copy-start.10 = (bf16[128,5120]{1,0:T(8,128)(2,1)S(1)}, bf16[128,5120]{1,0:T(8,128)(2,1)}, u32[]{:S(2)}) copy-start(bf16[128,5120]{1,0:T(8,128)(2,1)} %copy-done.9) | copy-start | bytes 3932164
  113.5 118.8 %copy-start.12 = (bf16[128,5120]{1,0:T(8,128)(2,1)}, bf16[128,5120]{1,0:T(8,128)(2,1)S(1)}, u32[]{:S(2)}) copy-start(bf16[128,5120]{1,0:T(8,128)(2,1)S(1)} %collective-permute-done.7) | copy-start | bytes 3932164
  115.5 75.5 %collective-permute-start.8 = (bf16[256,5120]{1,0:T(8,128)(2,1)S(1)}, bf16[256,5120]{1,0:T(8,128)(2,1)S(1)}, u32[]{:S(2)}, u32[]{:S(2)}) collective-permute-start(bf16[256,5120]{1,0:T(8,128)(2,1)S(1)} %pad_maximum_fusion.3), channel_id=1, source_target_pairs={{0,48},{1,17},{2,50},{3,19},{4,52},{5,21},{6,54},{7,23},{8,56},{9,... | collective-permute-start | bytes 7864328 | tf_op jit(solution)/shard_map/ppermute | solution.py:39
  116.9 46.0 %collective-permute-start.3 = (bf16[5120,192]{0,1:T(8,128)(2,1)S(1)}, bf16[5120,192]{0,1:T(8,128)(2,1)S(1)}, u32[]{:S(2)}, u32[]{:S(2)}) collective-permute-start(bf16[5120,192]{0,1:T(8,128)(2,1)S(1)} %bitcast.62), channel_id=1, source_target_pairs={{0,16},{1,49},{2,18},{3,51},{4,20},{5,53},{6,22},{7,55},{8,24},{9,... | collective-permute-start | bytes 5898248 | tf_op jit(solution)/shard_map/ppermute | solution.py:39
  118.8 72.2 %collective-permute-start.4 = (bf16[192,5120]{1,0:T(8,128)(2,1)S(1)}, bf16[192,5120]{1,0:T(8,128)(2,1)S(1)}, u32[]{:S(2)}, u32[]{:S(2)}) collective-permute-start(bf16[192,5120]{1,0:T(8,128)(2,1)S(1)} %bitcast.61), channel_id=1, source_target_pairs={{0,16},{1,49},{2,18},{3,51},{4,20},{5,53},{6,22},{7,55},{8,24},{9,... | collective-permute-start | bytes 5898248 | tf_op jit(solution)/shard_map/ppermute | solution.py:39
  119.6 92.5 %collective-permute-start.2 = (bf16[5120,192]{0,1:T(8,128)(2,1)S(1)}, bf16[5120,192]{0,1:T(8,128)(2,1)S(1)}, u32[]{:S(2)}, u32[]{:S(2)}) collective-permute-start(bf16[5120,192]{0,1:T(8,128)(2,1)S(1)} %bitcast.60), channel_id=1, source_target_pairs={{0,16},{1,49},{2,18},{3,51},{4,20},{5,53},{6,22},{7,55},{8,24},{9,... | collective-permute-start | bytes 5898248 | tf_op jit(solution)/shard_map/ppermute | solution.py:39
  162.9 66.2 %copy-start.19 = (bf16[256,5120]{1,0:T(8,128)(2,1)}, bf16[256,5120]{1,0:T(8,128)(2,1)S(1)}, u32[]{:S(2)}) copy-start(bf16[256,5120]{1,0:T(8,128)(2,1)S(1)} %collective-permute-done.1) | copy-start | bytes 7864324
  191.0 41.4 %copy-start.22 = (bf16[256,5120]{1,0:T(8,128)(2,1)}, bf16[256,5120]{1,0:T(8,128)(2,1)S(1)}, u32[]{:S(2)}) copy-start(bf16[256,5120]{1,0:T(8,128)(2,1)S(1)} %collective-permute-done.8) | copy-start | bytes 7864324
  215.4 22.9 %copy-start.16 = (bf16[512,192]{0,1:T(8,128)(2,1)}, bf16[512,192]{0,1:T(8,128)(2,1)S(1)}, u32[]{:S(2)}) copy-start(bf16[512,192]{0,1:T(8,128)(2,1)S(1)} %get-tuple-element.6) | copy-start | bytes 589828
  219.3 121.7 %collective-permute-start.13 = (bf16[192,5120]{1,0:T(8,128)(2,1)}, bf16[192,5120]{1,0:T(8,128)(2,1)}, u32[]{:S(2)}, u32[]{:S(2)}) collective-permute-start(bf16[192,5120]{1,0:T(8,128)(2,1)} %convolution_convert_fusion.4), channel_id=1, source_target_pairs={{0,16},{1,49},{2,18},{3,51},{4,20},{5,53},{6,22},{7,55},{8,24},{9,... | collective-permute-start | bytes 5898248 | tf_op jit(solution)/shard_map/ppermute | solution.py:39
  225.9 165.2 %collective-permute-start.12 = (bf16[5120,192]{0,1:T(8,128)(2,1)}, bf16[5120,192]{0,1:T(8,128)(2,1)}, u32[]{:S(2)}, u32[]{:S(2)}) collective-permute-start(bf16[5120,192]{0,1:T(8,128)(2,1)} %convolution_convert_fusion.2), channel_id=1, source_target_pairs={{0,16},{1,49},{2,18},{3,51},{4,20},{5,53},{6,22},{7,55},{8,24},{9,... | collective-permute-start | bytes 5898248 | tf_op jit(solution)/shard_map/ppermute | solution.py:39
  235.6 9.5 %copy-start.14 = (bf16[512,192]{0,1:T(8,128)(2,1)}, bf16[512,192]{0,1:T(8,128)(2,1)S(1)}, u32[]{:S(2)}) copy-start(bf16[512,192]{0,1:T(8,128)(2,1)S(1)} %get-tuple-element.11) | copy-start | bytes 589828
  240.7 50.2 %collective-permute-start.9 = (bf16[256,5120]{1,0:T(8,128)(2,1)}, bf16[256,5120]{1,0:T(8,128)(2,1)S(1)}, u32[]{:S(2)}, u32[]{:S(2)}) collective-permute-start(bf16[256,5120]{1,0:T(8,128)(2,1)} %fusion.5), channel_id=1, source_target_pairs={{0,48},{1,17},{2,50},{3,19},{4,52},{5,21},{6,54},{7,23},{8,56},{9,... | collective-permute-start | bytes 7864328 | tf_op jit(solution)/shard_map/ppermute | solution.py:39
  242.5 92.0 %collective-permute-start.5 = (bf16[256,5120]{1,0:T(8,128)(2,1)S(1)}, bf16[256,5120]{1,0:T(8,128)(2,1)}, u32[]{:S(2)}, u32[]{:S(2)}) collective-permute-start(bf16[256,5120]{1,0:T(8,128)(2,1)S(1)} %fusion.4), channel_id=1, source_target_pairs={{0,48},{1,17},{2,50},{3,19},{4,52},{5,21},{6,54},{7,23},{8,56},{9,... | collective-permute-start | bytes 7864328 | tf_op jit(solution)/shard_map/ppermute | solution.py:39
  247.0 44.0 %copy-start.17 = (bf16[512,192]{0,1:T(8,128)(2,1)S(1)}, bf16[512,192]{0,1:T(8,128)(2,1)}, u32[]{:S(2)}) copy-start(bf16[512,192]{0,1:T(8,128)(2,1)} %copy-done.16) | copy-start | bytes 589828
  292.0 1.7 copy-start.20
  292.2 53.8 %collective-permute-start.10 = (bf16[128,5120]{1,0:T(8,128)(2,1)S(1)}, bf16[128,5120]{1,0:T(8,128)(2,1)S(1)}, u32[]{:S(2)}, u32[]{:S(2)}) collective-permute-start(bf16[128,5120]{1,0:T(8,128)(2,1)S(1)} %slice.122), channel_id=1, source_target_pairs={{0,64},{1,65},{2,66},{3,67},{4,68},{5,69},{6,70},{7,71},{8,72},{9,... | collective-permute-start | bytes 3932168 | tf_op jit(solution)/shard_map/ppermute | solution.py:39
  297.6 98.9 %collective-permute-start.11 = (bf16[5120,192]{0,1:T(8,128)(2,1)}, bf16[5120,192]{0,1:T(8,128)(2,1)}, u32[]{:S(2)}, u32[]{:S(2)}) collective-permute-start(bf16[5120,192]{0,1:T(8,128)(2,1)} %convolution_convert_fusion.3), channel_id=1, source_target_pairs={{0,16},{1,49},{2,18},{3,51},{4,20},{5,53},{6,22},{7,55},{8,24},{9,... | collective-permute-start | bytes 5898248 | tf_op jit(solution)/shard_map/ppermute | solution.py:39
  334.5 6.5 %copy-start.23 = (bf16[256,5120]{1,0:T(8,128)(2,1)S(1)}, bf16[256,5120]{1,0:T(8,128)(2,1)}, u32[]{:S(2)}) copy-start(bf16[256,5120]{1,0:T(8,128)(2,1)} %copy-done.22) | copy-start | bytes 7864324
  337.4 2.3 copy-start.3
  339.8 1.8 copy-start.13
  339.8 1.8 copy-start.15
  341.0 24.2 %collective-permute-start.6 = (bf16[128,5120]{1,0:T(8,128)(2,1)}, bf16[128,5120]{1,0:T(8,128)(2,1)S(1)}, u32[]{:S(2)}, u32[]{:S(2)}) collective-permute-start(bf16[128,5120]{1,0:T(8,128)(2,1)} %slice.123), channel_id=1, source_target_pairs={{0,64},{1,65},{2,66},{3,67},{4,68},{5,69},{6,70},{7,71},{8,72},{9,... | collective-permute-start | bytes 3932168 | tf_op jit(solution)/shard_map/ppermute | solution.py:39
  347.4 36.5 %all-to-all-start.3 = ((bf16[16,8,5120]{2,1,0:T(8,128)(2,1)}), bf16[16,8,5120]{2,1,0:T(8,128)(2,1)S(1)}, u32[]{:S(2)}, u32[]{:S(2)}) async-start(bf16[16,8,5120]{2,1,0:T(8,128)(2,1)} %fusion.16), calls=%async_computation.3 | async-start | bytes 2621440 | tf_op jit(solution)/shard_map/all_to_all | solution.py:77
  368.4 22.7 %copy-start.11 = (bf16[128,5120]{1,0:T(8,128)(2,1)S(1)}, bf16[128,5120]{1,0:T(8,128)(2,1)}, u32[]{:S(2)}) copy-start(bf16[128,5120]{1,0:T(8,128)(2,1)} %copy-done.9) | copy-start | bytes 3932164
  383.9 12.7 %copy-start.7 = (bf16[16,8,5120]{2,1,0:T(8,128)(2,1)}, bf16[16,8,5120]{2,1,0:T(8,128)(2,1)S(1)}, u32[]{:S(2)}) copy-start(bf16[16,8,5120]{2,1,0:T(8,128)(2,1)S(1)} %all-to-all-done.3) | copy-start | bytes 3932164
  383.9 25.9 %all-to-all-start.1 = ((bf16[16,8,5120]{2,1,0:T(8,128)(2,1)}), bf16[16,8,5120]{2,1,0:T(8,128)(2,1)}, u32[]{:S(2)}, u32[]{:S(2)}) async-start(bf16[16,8,5120]{2,1,0:T(8,128)(2,1)} %fusion.15), calls=%async_computation.1 | async-start | bytes 2621440 | tf_op jit(solution)/shard_map/all_to_all | solution.py:77
  391.1 5.5 %copy-start.21 = (bf16[256,5120]{1,0:T(8,128)(2,1)S(1)}, bf16[256,5120]{1,0:T(8,128)(2,1)}, u32[]{:S(2)}) copy-start(bf16[256,5120]{1,0:T(8,128)(2,1)} %copy-done.19) | copy-start | bytes 7864324
  396.5 4.6 %copy-start.8 = (bf16[16,8,5120]{2,1,0:T(8,128)(2,1)S(1)}, bf16[16,8,5120]{2,1,0:T(8,128)(2,1)}, u32[]{:S(2)}) copy-start(bf16[16,8,5120]{2,1,0:T(8,128)(2,1)} %copy-done.7) | copy-start | bytes 3932164
  401.2 13.6 %copy-start.1 = (bf16[256,5120]{1,0:T(8,128)(2,1)S(1)}, bf16[256,5120]{1,0:T(8,128)(2,1)}, u32[]{:S(2)}) copy-start(bf16[256,5120]{1,0:T(8,128)(2,1)} %param.9) | copy-start | bytes 7864324

commit v2 on v0

v2 whole, which is shorter than its diff:
```python
import functools

import jax
import jax.numpy as jnp
from jax import lax
from jax.experimental import pallas as pl
from jax.experimental.pallas import tpu as pltpu
from jax.sharding import PartitionSpec as P

MESH = pl.DeviceIdType.MESH
F32 = jnp.float32
BF16 = jnp.bfloat16
STEP = 512


def dot(left, right, left_dim=1, right_dim=0):
    return lax.dot_general(
        left, right, (((left_dim,), (right_dim,)), ((), ())), preferred_element_type=F32
    )


def over(count, body):
    lax.fori_loop(0, count, lambda i, carry: (body(i), carry)[1], 0)


def columns(index, width, base=0):
    return pl.ds(pl.multiple_of(base + index * width, 128), width)


def layer(
    sizes,
    chosen_ref,
    scale_ref,
    tokens,
    cotangent,
    w_gate,
    w_up,
    w_down,
    moe_out,
    grad_tokens,
    grad_gate,
    grad_up,
    grad_down,
    gates,
    ups,
    downs,
    token_rows,
    grad_rows,
    sent_tokens,
    sent_grads,
    part_out,
    part_in,
    first_a,
    first_b,
    second_a,
    second_b,
    back_out,
    back_in,
    swap_from,
    swap_to,
    acts_t,
    acts,
    pre,
    pre_down,
    send_sems,
    recv_sems,
    local_sems,
):
    n_dp, n_expert, slot = sizes
    n_y = n_dp // 2
    d = lax.axis_index("dp")
    e = lax.axis_index("expert")
    x_hi, y = d // n_y, d % n_y
    core = e % 2
    near = (1 - 2 * core) * (1 - 2 * (y % 2))
    side_x = ((1 - x_hi) * n_y + y, e)
    side_y = (x_hi * n_y + (y - near + n_y) % n_y, e)
    side_w = (x_hi * n_y + (y + near + n_y) % n_y, e)
    peers = [(d, (e + k) % n_expert) for k in range(1, n_expert)]
    width = tokens.shape[1]
    token_count = tokens.shape[0]
    block = n_expert * slot
    all_rows = 4 * block
    shard = w_down.shape[0]
    both = 2 * shard
    cut = first_a.shape[2]
    rest = width - cut
    part_a, part_b = pl.ds(0, cut), pl.ds(cut, rest)

    counter = [0]

    def remote(source, target, device):
        i = counter[0]
        counter[0] += 1
        return pltpu.make_async_remote_copy(
            src_ref=source,
            dst_ref=target,
            send_sem=send_sems.at[i],
            recv_sem=recv_sems.at[i],
            device_id=device,
            device_id_type=MESH,
        )

    local_counter = [0]

    def local(source, target):
        i = local_counter[0]
        local_counter[0] += 1
        copy = pltpu.make_async_copy(source, target, local_sems.at[i])
        copy.start()
        return copy

    take_tokens = local(tokens, swap_from.at[pl.ds(0, token_count)])
    take_cotangent = local(cotangent, swap_from.at[pl.ds(token_count, token_count)])
    weights = ((w_gate, gates), (w_up, ups), (w_down, downs))
    take_weights = [local(own, held.at[pl.ds(0, shard)]) for own, held in weights]

    barrier = pltpu.get_barrier_semaphore()
    partners = peers + [side_x, side_y, side_w]
    for partner in partners:
        pl.semaphore_signal(barrier, inc=1, device_id=partner, device_id_type=MESH)
    pl.semaphore_wait(barrier, len(partners))

    swaps = [remote(own, held.at[pl.ds(shard, shard)], side_w) for own, held in weights]
    for copy in swaps:
        copy.start()

    def all_to_all(source, target):
        copies = [
            remote(source.at[pl.ds(peer[1] * slot, slot)], target.at[pl.ds(e * slot, slot)], peer)
            for peer in peers
        ]
        for copy in copies:
            copy.start()
        mine = local(source.at[pl.ds(e * slot, slot)], target.at[pl.ds(e * slot, slot)])
        return copies, mine

    def landed(group):
        for copy in group[0]:
            copy.wait_recv()
        group[1].wait()

    def wait_sends(copies):
        for copy in copies:
            copy.wait_send()

    token_ids = lax.broadcasted_iota(jnp.int32, (token_count, block), 0)
    named = jnp.where(token_ids == chosen_ref[...], 1.0, 0.0).astype(F32)
    picks = jnp.transpose(named).astype(BF16)
    scale_column = jnp.transpose(jnp.broadcast_to(scale_ref[...], (block, block)))[:, :1]

    take_tokens.wait()

    def pick_tokens(i):
        at = columns(i, STEP)
        sent_tokens[:, at] = dot(picks, swap_from[pl.ds(0, token_count), at]).astype(BF16)

    over(width // STEP, pick_tokens)
    out_tokens = all_to_all(sent_tokens, token_rows)
    take_cotangent.wait()

    def pick_grads(i):
        at = columns(i, STEP)
        rows = dot(picks, swap_from[pl.ds(token_count, token_count), at])
        sent_grads[:, at] = (rows * scale_column).astype(BF16)

    over(width // STEP, pick_grads)
    out_grads = all_to_all(sent_grads, grad_rows)

    def block_of(i, n=1):
        return pl.ds(i * block, n * block)

    def spread(rows):
        to_x = remote(rows.at[block_of(0)], rows.at[block_of(1)], side_x)
        to_y = remote(rows.at[block_of(0)], rows.at[block_of(2)], side_y)
        on_y = remote(rows.at[block_of(1), part_a], rows.at[block_of(3), part_a], side_y)
        on_x = remote(rows.at[block_of(2), part_b], rows.at[block_of(3), part_b], side_x)
        return to_x, to_y, on_y, on_x

    def relay(group):
        to_x, to_y, on_y, on_x = group
        to_y.wait_recv()
        on_x.start()
        to_x.wait_recv()
        on_y.start()

    landed(out_tokens)
    token_spread = spread(token_rows)
    token_spread[0].start()
    token_spread[1].start()
    relay(token_spread)
    landed(out_grads)
    grad_spread = spread(grad_rows)
    grad_spread[0].start()
    grad_spread[1].start()

    deep = 2 * STEP

    def project(target, weight, side, rows):
        target[...] = jnp.zeros(target.shape, F32)

        def one(i):
            at = columns(i, deep)
            target[...] += dot(weight[pl.ds(side * shard, shard), at], rows[:, at], 1, 1)

        over(width // deep, one)

    for copy in take_weights:
        copy.wait()
    token_spread[2].wait_recv()
    token_spread[3].wait_recv()
    own, other = pl.ds(0, shard), pl.ds(shard, shard)
    project(pre.at[0, own], gates, 0, token_rows)
    project(pre.at[1, own], ups, 0, token_rows)
    swaps[0].wait_recv()
    project(pre.at[0, other], gates, 1, token_rows)
    swaps[1].wait_recv()
    project(pre.at[1, other], ups, 1, token_rows)

    def keep(which, at, value):
        acts_t[which, at] = value.astype(BF16)
        acts[which, :, at] = jnp.transpose(value).astype(BF16)

    for i in range(both // 128):
        at = pl.ds(i * 128, 128)
        gate_value = pre[0, at]
        keep(2, at, gate_value * jax.nn.sigmoid(gate_value) * pre[1, at])

    relay(grad_spread)

    def give(parts, terms, stream):
        def one(i):
            at = columns(i, STEP)
            total = dot(acts[terms[0][0]], terms[0][1][:, at])
            for which, weight in terms[1:]:
                total += dot(acts[which], weight[:, at])
            parts[:, at] = total.astype(BF16)

        over(cut // STEP, one)
        near_y = remote(parts.at[block_of(2, 2), part_a], first_a.at[stream], side_y)
        near_y.start()
        over(rest // STEP, lambda i: one(i + cut // STEP))
        me_x = remote(parts.at[block_of(1), part_b], first_b.at[stream, block_of(0)], side_x)
        far_x = remote(parts.at[block_of(3), part_b], first_b.at[stream, block_of(1)], side_x)
        me_x.start()
        far_x.start()
        return near_y, me_x, far_x

    def add_on(parts, near, stream):
        near_y, me_x, far_x = near
        near_y.wait_recv()

        def one(i):
            at = columns(i, STEP)
            total = parts[block_of(1), at].astype(F32) + first_a[stream, block_of(1), at].astype(F32)
            first_a[stream, block_of(1), at] = total.astype(BF16)

        over(cut // STEP, one)
        on_x = remote(first_a.at[stream, block_of(1)], second_a.at[stream], side_x)
        on_x.start()
        far_x.wait_recv()

        def two(i):
            at = columns(i, STEP)
            of = columns(i, STEP, cut)
            total = parts[block_of(2), of].astype(F32) + first_b[stream, block_of(1), at].astype(F32)
            first_b[stream, block_of(1), at] = total.astype(BF16)

        over(rest // STEP, two)
        on_y = remote(first_b.at[stream, block_of(1)], second_b.at[stream], side_y)
        on_y.start()
        me_x.wait_recv()
        return on_x, on_y

    def finish(parts, on, sums, stream):
        on_x, on_y = on
        on_x.wait_recv()

        def one(i):
            at = columns(i, STEP)
            total = parts[block_of(0), at].astype(F32) + first_a[stream, block_of(0), at].astype(F32)
            sums[:, at] = (total + second_a[stream, :, at].astype(F32)).astype(BF16)

        over(cut // STEP, one)
        on_y.wait_recv()

        def two(i):
            at = columns(i, STEP)
            of = columns(i, STEP, cut)
            total = parts[block_of(0), of].astype(F32) + first_b[stream, block_of(0), at].astype(F32)
            sums[:, of] = (total + second_b[stream, :, at].astype(F32)).astype(BF16)

        over(rest // STEP, two)

    swaps[2].wait_recv()
    near_out = give(part_out, [(2, downs)], 0)

    grad_spread[2].wait_recv()
    grad_spread[3].wait_recv()

    def slab(which):
        return pl.ds(which * shard, shard)

    def swap_grad(which, rows):
        def one(i):
            at = columns(i, STEP)
            swap_from[slab(which), at] = dot(acts_t[which, other], rows[:, at]).astype(BF16)

        over(width // STEP, one)
        copy = remote(swap_from.at[slab(which)], swap_to.at[slab(which)], side_w)
        copy.start()
        return copy

    def own_grad(which, rows, copy, target):
        copy.wait_recv()

        def one(i):
            at = columns(i, STEP)
            total = dot(acts_t[which, own], rows[:, at]) + swap_to[slab(which), at].astype(F32)
            swap_to[slab(which), at] = total.astype(BF16)

        over(width // STEP, one)
        return local(swap_to.at[slab(which)], target)

    swap_down = swap_grad(2, grad_rows)
    project(pre_down.at[own], downs, 0, grad_rows)
    project(pre_down.at[other], downs, 1, grad_rows)

    for i in range(both // 128):
        at = pl.ds(i * 128, 128)
        gate_value, upward, hidden_grad = pre[0, at], pre[1, at], pre_down[at]
        sigma = jax.nn.sigmoid(gate_value)
        keep(0, at, hidden_grad * upward * (sigma * (1.0 + gate_value * (1.0 - sigma))))
        keep(1, at, hidden_grad * (gate_value * sigma))

    near_in = give(part_in, [(0, gates), (1, ups)], 1)
    on_out = add_on(part_out, near_out, 0)
    swap_gate = swap_grad(0, token_rows)
    swap_up = swap_grad(1, token_rows)
    wait_sends(out_tokens[0])
    finish(part_out, on_out, sent_tokens, 0)
    home_out = all_to_all(sent_tokens, back_out)
    on_in = add_on(part_in, near_in, 1)
    writes = [own_grad(2, grad_rows, swap_down, grad_down)]

    def merge(table, arrived, parts, near, target):
        wait_sends(near)
        coarse = table.astype(BF16)
        fine = (table - coarse.astype(F32)).astype(BF16)

        def one(i):
            at = columns(i, STEP)
            total = dot(coarse, arrived[:, at]) + dot(fine, arrived[:, at])
            parts[pl.ds(0, token_count), at] = total.astype(BF16)

        over(width // STEP, one)
        return local(parts.at[pl.ds(0, token_count)], target)

    wait_sends(out_grads[0])
    finish(part_in, on_in, sent_grads, 1)
    home_in = all_to_all(sent_grads, back_in)
    landed(home_out)
    named = jnp.where(token_ids == chosen_ref[...], 1.0, 0.0).astype(F32)
    writes.append(merge(named * scale_ref[...], back_out, part_out, near_out, moe_out))
    writes.append(own_grad(0, token_rows, swap_gate, grad_gate))
    writes.append(own_grad(1, token_rows, swap_up, grad_up))
    landed(home_in)
    wait_sends(near_in)
    only = named.astype(BF16)

    def merge_grads(i):
        at = columns(i, STEP)
        part_in[pl.ds(0, token_count), at] = dot(only, back_in[:, at]).astype(BF16)

    over(width // STEP, merge_grads)
    writes.append(local(part_in.at[pl.ds(0, token_count)], grad_tokens))

    wait_sends(swaps + list(token_spread) + list(grad_spread) + list(on_out) + list(on_in))
    wait_sends([swap_down, swap_gate, swap_up] + home_out[0] + home_in[0])
    for copy in writes:
        copy.wait()


def on_device(tokens, cotangent, slot_token, slot_weight, w_gate, w_up, w_down):
    n_dp, n_expert = lax.axis_size("dp"), lax.axis_size("expert")
    slot = slot_token.shape[2]
    block = n_expert * slot
    token_count, width = tokens.shape
    shard = w_down.shape[1]
    cut = width * 3 // 5
    rest = width - cut
    gate_t = jnp.swapaxes(w_gate[0], 0, 1)
    up_t = jnp.swapaxes(w_up[0], 0, 1)
    whole = pl.BlockSpec(memory_space=pl.ANY)
    small = pl.BlockSpec(memory_space=pltpu.VMEM)
    weights = pltpu.VMEM((2 * shard, width), BF16)
    rows = pltpu.VMEM((4 * block, width), BF16)
    one = pltpu.VMEM((block, width), BF16)
    copies = 3 + 4 * (n_expert - 1) + 8 + 10 + 3
    results = pl.pallas_call(
        functools.partial(layer, (n_dp, n_expert, slot)),
        out_shape=[
            jax.ShapeDtypeStruct((token_count, width), BF16),
            jax.ShapeDtypeStruct((token_count, width), BF16),
            jax.ShapeDtypeStruct((shard, width), BF16),
            jax.ShapeDtypeStruct((shard, width), BF16),
            jax.ShapeDtypeStruct((shard, width), BF16),
        ],
        in_specs=[small, small] + [whole] * 5,
        out_specs=[whole] * 5,
        scratch_shapes=[
            weights,
            weights,
            weights,
            rows,
            rows,
            one,
            one,
            rows,
            rows,
            pltpu.VMEM((2, 2 * block, cut), BF16),
            pltpu.VMEM((2, 2 * block, rest), BF16),
            pltpu.VMEM((2, block, cut), BF16),
            pltpu.VMEM((2, block, rest), BF16),
            one,
            one,
            pltpu.VMEM((3 * shard, width), BF16),
            pltpu.VMEM((3 * shard, width), BF16),
            pltpu.VMEM((3, 2 * shard, 4 * block), BF16),
            pltpu.VMEM((3, 4 * block, 2 * shard), BF16),
            pltpu.VMEM((2, 2 * shard, 4 * block), F32),
            pltpu.VMEM((2 * shard, 4 * block), F32),
            pltpu.SemaphoreType.DMA((copies,)),
            pltpu.SemaphoreType.DMA((copies,)),
            pltpu.SemaphoreType.DMA((14,)),
        ],
        compiler_params=pltpu.CompilerParams(
            collective_id=0, has_side_effects=True, vmem_limit_bytes=67043328
        ),
        name="layer",
    )(
        slot_token.reshape(1, block),
        slot_weight.reshape(1, block),
        tokens,
        cotangent,
        gate_t,
        up_t,
        w_down[0],
    )
    moe_out, grad_tokens, grad_gate, grad_up, grad_down = results
    return (
        moe_out,
        grad_tokens,
        jnp.swapaxes(grad_gate, 0, 1)[None],
        jnp.swapaxes(grad_up, 0, 1)[None],
        grad_down[None],
    )


def solution(mesh):
    in_specs = (
        P(("dp", "expert"), None),
        P(("dp", "expert"), None),
        P(("dp", "expert"), None, None),
        P(("dp", "expert"), None, None),
        P("expert", None, "dp"),
        P("expert", None, "dp"),
        P("expert", "dp", None),
    )
    out_specs = (
        P(("dp", "expert"), None),
        P(("dp", "expert"), None),
        P("expert", None, "dp"),
        P("expert", None, "dp"),
        P("expert", "dp", None),
    )
    return jax.shard_map(
        on_device, mesh=mesh, in_specs=in_specs, out_specs=out_specs, check_vma=False
    )
```

time: 623 us -> 261 us (0.42)
  waiting for transfers between devices: 442 us -> 0 us
  Pallas kernels: 0 us -> 245 us
  matrix products: 83.4 us -> 0 us
  blocking collectives: 60.4 us -> 0 us
  between operations: 13.9 us -> 0.65 us
  starting transfers between devices: 12.3 us -> 0 us
  local copies, waits for them, and re-layouts: 6.59 us -> 14.5 us
    pallas_call x0 -> x1, Pallas kernels: none -> 245 us  [on_device(): pl.pallas_call(functools.partial(layer, (n_dp, n_expert, slot)), out_shap...]
    reduce_scatter x2 -> x0, waiting for transfers between devices: 234 us -> none  [collect(): lax.psum_scatter(term_of(jnp.int32(0), own_rows * lax.axis_size('dp')).as...]
    all_gather x2 -> x0, waiting for transfers between devices: 208 us -> none  [the longest x1 110 us: dispatch(): lax.all_gather(landed[1], 'dp', axis=0, tiled=True)]
    dot_general x11 -> x0, matrix products: 83.4 us -> none  [the longest x1 12.1 us: input_term(): jnp.einsum('rf,df->rd', upward_grad, local_up, preferred_element_type=jnp...]
    all_to_all x2 -> x0, blocking collectives: 60.4 us -> none  [the longest x1 34.1 us: dispatch(): lax.all_to_all(sent_grads, 'expert', split_axis=0, concat_axis=0, tiled=T...]
    all_to_all x2 -> x0, starting transfers between devices: 11.7 us -> none  [collect(): lax.all_to_all(summed, 'expert', split_axis=0, concat_axis=0, tiled=True)]
    unnamed x18 -> x15, local copies, waits for them, and re-layouts: 1.69 us -> 13.3 us
  transfers between devices with their start and end apart: 6 -> 0, of which waited for: 4 -> 0; matrix products, arithmetic and copies ran while one was open for 11% -> 0% of each run, Pallas kernels for 0% -> 0%
where the time goes in v2:
time: 261 us; the launch traced here: 260 us
  Pallas kernels  245 us (94%)
  local copies, waits for them, and re-layouts  14.5 us (6%)
    pallas_call x1, Pallas kernels, on_device(): pl.pallas_call(functools.partial(layer, (n_dp, n_expert, slot)), out_shap...  245 us
    unnamed x15, local copies, waits for them, and re-layouts  13.3 us

profile of v2, /device:TPU:1, one launch (start us, length us, event | category | flops | bytes accessed | tf_op | source)
XLA Modules:
  0.0 260.3 jit_solution(3478832920107006036)
XLA Ops:
  0.6 0.8 copy.14
  1.4 0.6 reshape.16.chosen_ref
  2.0 0.8 copy.15
  2.7 0.6 reshape.17.scale_ref
  3.4 245.1 %layer.1 = (bf16[256,5120]{1,0:T(8,128)(2,1)}, bf16[256,5120]{1,0:T(8,128)(2,1)}, bf16[192,5120]{1,0:T(8,128)(2,1)}, bf16[192,5120]{1,0:T(8,128)(2,1)}, bf16[192,5120]{1,0:T(8,128)(2,1)}) custom-call(s32[1,128]{1,0:T(1,128)} %reshape.16.chosen_ref, f32[1,128]{1,0:T(1,128)} %reshape.17.scale_ref, bf16[256,5120]{1,0:T(8,128)(2,1)} %tokens.1, ...), custom_call_target="tpu_custom_call" | custom-call | tf_op jit(solution)/shard_map/layer/pallas_call | solution.py:400
  248.5 0.0 copy-start
  248.5 3.6 %copy.21 = bf16[256,5120]{1,0:T(8,128)(2,1)} copy(bf16[256,5120]{1,0:T(8,128)(2,1)} %get-tuple-element.20) | data formatting | bytes 5242880
  252.0 0.0 copy-done
  252.0 0.0 copy-start.3
  252.0 1.5 copy.22
  253.5 1.0 copy-done.3
  254.5 0.0 copy-start.2
  254.5 1.3 copy.23
  255.8 1.0 copy-done.2
  256.8 0.0 copy-start.1
  256.8 1.3 copy.24
  258.1 1.0 copy-done.1
  259.0 1.3 copy.25
Async XLA Ops:
  248.5 3.6 %copy-start = (bf16[256,5120]{1,0:T(8,128)(2,1)S(1)}, bf16[256,5120]{1,0:T(8,128)(2,1)}, u32[]{:S(2)}) copy-start(bf16[256,5120]{1,0:T(8,128)(2,1)} %get-tuple-element.21) | copy-start | bytes 7864324
  252.0 2.5 copy-start.3
  254.5 2.3 copy-start.2
  256.8 2.3 copy-start.1

commit v3 on v2

--- a/solution.py
+++ b/solution.py
@@ -27,20 +27,38 @@
     return pl.ds(pl.multiple_of(base + index * width, 128), width)
 
 
+def flat(table):
+    slot, n_expert = table.shape
+    row = lax.broadcasted_iota(jnp.int32, (slot, n_expert * slot), 0)
+    lane = lax.broadcasted_iota(jnp.int32, (slot, n_expert * slot), 1)
+    wide = jnp.zeros(lane.shape, table.dtype)
+    for j in range(n_expert):
+        wide = jnp.where(lane == j * slot + row, table[:, j : j + 1], wide)
+    return jnp.sum(wide, axis=0, keepdims=True)
+
+
+def names(chosen, token_count):
+    block = chosen.shape[1]
+    token_ids = lax.broadcasted_iota(jnp.int32, (token_count, block), 0)
+    return jnp.where(token_ids == chosen, 1.0, 0.0).astype(F32)
+
+
 def layer(
     sizes,
-    chosen_ref,
-    scale_ref,
+    chosen_in,
+    scale_in,
     tokens,
     cotangent,
     w_gate,
     w_up,
     w_down,
-    moe_out,
-    grad_tokens,
+    back_out,
+    back_in,
     grad_gate,
     grad_up,
     grad_down,
+    chosen_ref,
+    scale_ref,
     gates,
     ups,
     downs,
@@ -54,8 +72,6 @@
     first_b,
     second_a,
     second_b,
-    back_out,
-    back_in,
     swap_from,
     swap_to,
     acts_t,
@@ -110,6 +126,7 @@
         copy.start()
         return copy
 
+    take_table = [local(chosen_in, chosen_ref), local(scale_in, scale_ref)]
     take_tokens = local(tokens, swap_from.at[pl.ds(0, token_count)])
     take_cotangent = local(cotangent, swap_from.at[pl.ds(token_count, token_count)])
     weights = ((w_gate, gates), (w_up, ups), (w_down, downs))
@@ -144,10 +161,10 @@
         for copy in copies:
             copy.wait_send()
 
-    token_ids = lax.broadcasted_iota(jnp.int32, (token_count, block), 0)
-    named = jnp.where(token_ids == chosen_ref[...], 1.0, 0.0).astype(F32)
-    picks = jnp.transpose(named).astype(BF16)
-    scale_column = jnp.transpose(jnp.broadcast_to(scale_ref[...], (block, block)))[:, :1]
+    for copy in take_table:
+        copy.wait()
+    picks = jnp.transpose(names(flat(chosen_ref[...]), token_count)).astype(BF16)
+    scale_column = jnp.transpose(jnp.broadcast_to(flat(scale_ref[...]), (block, block)))[:, :1]
 
     take_tokens.wait()
 
@@ -343,40 +360,72 @@
     on_in = add_on(part_in, near_in, 1)
     writes = [own_grad(2, grad_rows, swap_down, grad_down)]
 
-    def merge(table, arrived, parts, near, target):
-        wait_sends(near)
-        coarse = table.astype(BF16)
-        fine = (table - coarse.astype(F32)).astype(BF16)
-
-        def one(i):
-            at = columns(i, STEP)
-            total = dot(coarse, arrived[:, at]) + dot(fine, arrived[:, at])
-            parts[pl.ds(0, token_count), at] = total.astype(BF16)
-
-        over(width // STEP, one)
-        return local(parts.at[pl.ds(0, token_count)], target)
-
     wait_sends(out_grads[0])
     finish(part_in, on_in, sent_grads, 1)
     home_in = all_to_all(sent_grads, back_in)
-    landed(home_out)
-    named = jnp.where(token_ids == chosen_ref[...], 1.0, 0.0).astype(F32)
-    writes.append(merge(named * scale_ref[...], back_out, part_out, near_out, moe_out))
     writes.append(own_grad(0, token_rows, swap_gate, grad_gate))
     writes.append(own_grad(1, token_rows, swap_up, grad_up))
+    landed(home_out)
     landed(home_in)
-    wait_sends(near_in)
-    only = named.astype(BF16)
-
-    def merge_grads(i):
-        at = columns(i, STEP)
-        part_in[pl.ds(0, token_count), at] = dot(only, back_in[:, at]).astype(BF16)
-
-    over(width // STEP, merge_grads)
-    writes.append(local(part_in.at[pl.ds(0, token_count)], grad_tokens))
+    wait_sends(near_out + near_in)
 
     wait_sends(swaps + list(token_spread) + list(grad_spread) + list(on_out) + list(on_in))
     wait_sends([swap_down, swap_gate, swap_up] + home_out[0] + home_in[0])
+    for copy in writes:
+        copy.wait()
+
+
+PIECES = 4
+
+
+def merge(
+    chosen_ref,
+    scale_ref,
+    back_out,
+    back_in,
+    *refs,
+):
+    grads, (moe_out, grad_tokens), grads_out = refs[:3], refs[3:5], refs[5:8]
+    arrived, merged, held, in_sems, out_sems = refs[8:]
+    token_count, width = moe_out.shape
+    deep = width // (PIECES + 1)
+    tall = grads[0].shape[0] // PIECES
+    reads, jobs = [], []
+
+    def read(source, target):
+        copy = pltpu.make_async_copy(source, target, in_sems.at[len(reads)])
+        copy.start()
+        reads.append(copy)
+
+    for which, back in enumerate((back_out, back_in)):
+        for i in range(width // deep):
+            at = pl.ds(i * deep, deep)
+            read(back.at[:, at], arrived.at[which, :, at])
+            target = (moe_out, grad_tokens)[which].at[:, at]
+            jobs.append((which, i, merged.at[which, :, at], target))
+    for which, grad in enumerate(grads):
+        for i in range(PIECES):
+            at = pl.ds(i * tall, tall)
+            read(grad.at[at], held.at[which, at])
+            jobs.append((None, i, held.at[which, at], grads_out[which].at[at]))
+
+    named = names(flat(chosen_ref[...]), token_count)
+    table = named * flat(scale_ref[...])
+    coarse = table.astype(BF16)
+    fine = (table - coarse.astype(F32)).astype(BF16)
+    only = named.astype(BF16)
+    writes = []
+    for n, (which, i, source, target) in enumerate(jobs):
+        reads[n].wait()
+        if which is not None:
+            for half in range(2):
+                at = pl.ds(i * deep + half * (deep // 2), deep // 2)
+                rows = arrived[which, :, at]
+                total = dot(only, rows) if which else dot(coarse, rows) + dot(fine, rows)
+                merged[which, :, at] = total.astype(BF16)
+        copy = pltpu.make_async_copy(source, target, out_sems.at[n])
+        copy.start()
+        writes.append(copy)
     for copy in writes:
         copy.wait()
 
@@ -391,6 +440,7 @@
     rest = width - cut
     gate_t = jnp.swapaxes(w_gate[0], 0, 1)
     up_t = jnp.swapaxes(w_up[0], 0, 1)
+    chosen, scale = (jnp.swapaxes(table[0], 0, 1) for table in (slot_token, slot_weight))
     whole = pl.BlockSpec(memory_space=pl.ANY)
     small = pl.BlockSpec(memory_space=pltpu.VMEM)
     weights = pltpu.VMEM((2 * shard, width), BF16)
@@ -400,15 +450,17 @@
     results = pl.pallas_call(
         functools.partial(layer, (n_dp, n_expert, slot)),
         out_shape=[
-            jax.ShapeDtypeStruct((token_count, width), BF16),
-            jax.ShapeDtypeStruct((token_count, width), BF16),
+            jax.ShapeDtypeStruct((block, width), BF16),
+            jax.ShapeDtypeStruct((block, width), BF16),
             jax.ShapeDtypeStruct((shard, width), BF16),
             jax.ShapeDtypeStruct((shard, width), BF16),
             jax.ShapeDtypeStruct((shard, width), BF16),
         ],
-        in_specs=[small, small] + [whole] * 5,
+        in_specs=[whole] * 7,
         out_specs=[whole] * 5,
         scratch_shapes=[
+            pltpu.VMEM((slot, n_expert), jnp.int32),
+            pltpu.VMEM((slot, n_expert), F32),
             weights,
             weights,
             weights,
@@ -422,8 +474,6 @@
             pltpu.VMEM((2, 2 * block, rest), BF16),
             pltpu.VMEM((2, block, cut), BF16),
             pltpu.VMEM((2, block, rest), BF16),
-            one,
-            one,
             pltpu.VMEM((3 * shard, width), BF16),
             pltpu.VMEM((3 * shard, width), BF16),
             pltpu.VMEM((3, 2 * shard, 4 * block), BF16),
@@ -439,14 +489,31 @@
         ),
         name="layer",
     )(
-        slot_token.reshape(1, block),
-        slot_weight.reshape(1, block),
+        chosen,
+        scale,
         tokens,
         cotangent,
         gate_t,
         up_t,
         w_down[0],
     )
+    moved = 2 * (PIECES + 1) + 3 * PIECES
+    results = pl.pallas_call(
+        merge,
+        out_shape=[jax.ShapeDtypeStruct((token_count, width), BF16)] * 2
+        + [jax.ShapeDtypeStruct((shard, width), BF16)] * 3,
+        in_specs=[small] * 2 + [whole] * 5,
+        out_specs=[whole] * 5,
+        scratch_shapes=[
+            pltpu.VMEM((2, block, width), BF16),
+            pltpu.VMEM((2, token_count, width), BF16),
+            pltpu.VMEM((3, shard, width), BF16),
+            pltpu.SemaphoreType.DMA((moved,)),
+            pltpu.SemaphoreType.DMA((moved,)),
+        ],
+        compiler_params=pltpu.CompilerParams(vmem_limit_bytes=67043328),
+        name="merge",
+    )(chosen, scale, *results)
     moe_out, grad_tokens, grad_gate, grad_up, grad_down = results
     return (
         moe_out,

time: 261 us -> 250 us (0.958)
  local copies, waits for them, and re-layouts: 14.5 us -> 0 us
  Pallas kernels: 245 us -> 249 us
    unnamed x15 -> x0, local copies, waits for them, and re-layouts: 13.3 us -> none
    pallas_call x0 -> x1, Pallas kernels: none -> 8.14 us  [on_device(): pl.pallas_call(merge, out_shape=[jax.ShapeDtypeStruct((token_count, width...]
    pallas_call x1, Pallas kernels: 245 us -> 241 us  [on_device(): pl.pallas_call(functools.partial(layer, (n_dp, n_expert, slot)), out_shap...]
where the time goes in v3:
time: 250 us
  Pallas kernels  249 us (100%)
    pallas_call x1, Pallas kernels, on_device(): pl.pallas_call(functools.partial(layer, (n_dp, n_expert, slot)), out_shap...  241 us
    pallas_call x1, Pallas kernels, on_device(): pl.pallas_call(merge, out_shape=[jax.ShapeDtypeStruct((token_count, width...  8.14 us

profile of v3, /device:TPU:1, one launch (start us, length us, event | category | flops | bytes accessed | tf_op | source)
XLA Modules:
  0.0 250.0 jit_solution(17511293639851886001)
XLA Ops:
  0.6 241.2 %layer.1 = (bf16[128,5120]{1,0:T(8,128)(2,1)}, bf16[128,5120]{1,0:T(8,128)(2,1)}, bf16[192,5120]{1,0:T(8,128)(2,1)}, bf16[192,5120]{1,0:T(8,128)(2,1)}, bf16[192,5120]{1,0:T(8,128)(2,1)}) custom-call(s32[8,16]{1,0:T(8,128)} %bitcast.23, f32[8,16]{1,0:T(8,128)} %bitcast.25, bf16[256,5120]{1,0:T(8,128)(2,1)} %tokens.1, bf16[256,5120]{1,0:T(8,128)(2,1)} %cotangent.1, ...), custom_call_target="tpu_custom_call" | custom-call | tf_op jit(solution)/shard_map/layer/pallas_call | solution.py:450
  241.9 8.1 %merge.1 = (bf16[256,5120]{1,0:T(8,128)(2,1)}, bf16[256,5120]{1,0:T(8,128)(2,1)}, bf16[192,5120]{1,0:T(8,128)(2,1)}, bf16[192,5120]{1,0:T(8,128)(2,1)}, bf16[192,5120]{1,0:T(8,128)(2,1)}) custom-call(s32[8,16]{1,0:T(8,128)} %bitcast.24, f32[8,16]{1,0:T(8,128)} %bitcast.26, bf16[128,5120]{1,0:T(8,128)(2,1)} %get-tuple-element.15.back_out, ...), custom_call_target="tpu_custom_call" | custom-call | tf_op jit(solution)/shard_map/merge/pallas_call | solution.py:501

commit v4 on v3

--- a/solution.py
+++ b/solution.py
@@ -54,6 +54,8 @@
     w_down,
     back_out,
     back_in,
+    far_out,
+    far_in,
     grad_gate,
     grad_up,
     grad_down,
@@ -70,7 +72,6 @@
     part_in,
     first_a,
     first_b,
-    second_a,
     second_b,
     swap_from,
     swap_to,
@@ -93,6 +94,7 @@
     side_y = (x_hi * n_y + (y - near + n_y) % n_y, e)
     side_w = (x_hi * n_y + (y + near + n_y) % n_y, e)
     peers = [(d, (e + k) % n_expert) for k in range(1, n_expert)]
+    far_peers = [(side_x[0], (e + k) % n_expert) for k in range(n_expert)]
     width = tokens.shape[1]
     token_count = tokens.shape[0]
     block = n_expert * slot
@@ -133,7 +135,7 @@
     take_weights = [local(own, held.at[pl.ds(0, shard)]) for own, held in weights]
 
     barrier = pltpu.get_barrier_semaphore()
-    partners = peers + [side_x, side_y, side_w]
+    partners = peers + far_peers + [side_y, side_w]
     for partner in partners:
         pl.semaphore_signal(barrier, inc=1, device_id=partner, device_id_type=MESH)
     pl.semaphore_wait(barrier, len(partners))
@@ -142,20 +144,23 @@
     for copy in swaps:
         copy.start()
 
-    def all_to_all(source, target):
+    def all_to_all(source, target, to=peers):
         copies = [
             remote(source.at[pl.ds(peer[1] * slot, slot)], target.at[pl.ds(e * slot, slot)], peer)
-            for peer in peers
+            for peer in to
         ]
         for copy in copies:
             copy.start()
+        if to is far_peers:
+            return copies, None
         mine = local(source.at[pl.ds(e * slot, slot)], target.at[pl.ds(e * slot, slot)])
         return copies, mine
 
     def landed(group):
         for copy in group[0]:
             copy.wait_recv()
-        group[1].wait()
+        if group[1] is not None:
+            group[1].wait()
 
     def wait_sends(copies):
         for copy in copies:
@@ -166,6 +171,14 @@
     picks = jnp.transpose(names(flat(chosen_ref[...]), token_count)).astype(BF16)
     scale_column = jnp.transpose(jnp.broadcast_to(flat(scale_ref[...]), (block, block)))[:, :1]
 
+    def block_of(i, n=1):
+        return pl.ds(i * block, n * block)
+
+    def deal(sent, rows):
+        near_group = all_to_all(sent, rows.at[block_of(0)])
+        far_from, far_to = sent.at[:, part_a], rows.at[block_of(1), part_a]
+        return near_group, all_to_all(far_from, far_to, far_peers)
+
     take_tokens.wait()
 
     def pick_tokens(i):
@@ -173,7 +186,7 @@
         sent_tokens[:, at] = dot(picks, swap_from[pl.ds(0, token_count), at]).astype(BF16)
 
     over(width // STEP, pick_tokens)
-    out_tokens = all_to_all(sent_tokens, token_rows)
+    out_tokens = deal(sent_tokens, token_rows)
     take_cotangent.wait()
 
     def pick_grads(i):
@@ -182,34 +195,29 @@
         sent_grads[:, at] = (rows * scale_column).astype(BF16)
 
     over(width // STEP, pick_grads)
-    out_grads = all_to_all(sent_grads, grad_rows)
-
-    def block_of(i, n=1):
-        return pl.ds(i * block, n * block)
-
-    def spread(rows):
-        to_x = remote(rows.at[block_of(0)], rows.at[block_of(1)], side_x)
-        to_y = remote(rows.at[block_of(0)], rows.at[block_of(2)], side_y)
+    out_grads = deal(sent_grads, grad_rows)
+
+    def spread(rows, dealt):
+        to_y_b = remote(rows.at[block_of(0), part_b], rows.at[block_of(2), part_b], side_y)
+        to_y_a = remote(rows.at[block_of(0), part_a], rows.at[block_of(2), part_a], side_y)
+        to_x = remote(rows.at[block_of(0), part_b], rows.at[block_of(1), part_b], side_x)
         on_y = remote(rows.at[block_of(1), part_a], rows.at[block_of(3), part_a], side_y)
         on_x = remote(rows.at[block_of(2), part_b], rows.at[block_of(3), part_b], side_x)
-        return to_x, to_y, on_y, on_x
+        landed(dealt[0])
+        to_y_b.start()
+        to_y_a.start()
+        to_x.start()
+        landed(dealt[1])
+        on_y.start()
+        return to_y_b, to_y_a, to_x, on_y, on_x
 
     def relay(group):
-        to_x, to_y, on_y, on_x = group
-        to_y.wait_recv()
-        on_x.start()
-        to_x.wait_recv()
-        on_y.start()
-
-    landed(out_tokens)
-    token_spread = spread(token_rows)
-    token_spread[0].start()
-    token_spread[1].start()
+        group[0].wait_recv()
+        group[4].start()
+
+    token_spread = spread(token_rows, out_tokens)
     relay(token_spread)
-    landed(out_grads)
-    grad_spread = spread(grad_rows)
-    grad_spread[0].start()
-    grad_spread[1].start()
+    grad_spread = spread(grad_rows, out_grads)
 
     deep = 2 * STEP
 
@@ -224,8 +232,8 @@
 
     for copy in take_weights:
         copy.wait()
-    token_spread[2].wait_recv()
-    token_spread[3].wait_recv()
+    for copy in token_spread[1:]:
+        copy.wait_recv()
     own, other = pl.ds(0, shard), pl.ds(shard, shard)
     project(pre.at[0, own], gates, 0, token_rows)
     project(pre.at[1, own], ups, 0, token_rows)
@@ -263,18 +271,19 @@
         far_x.start()
         return near_y, me_x, far_x
 
-    def add_on(parts, near, stream):
+    def add_on(parts, near, back, far, stream):
         near_y, me_x, far_x = near
         near_y.wait_recv()
 
         def one(i):
             at = columns(i, STEP)
-            total = parts[block_of(1), at].astype(F32) + first_a[stream, block_of(1), at].astype(F32)
-            first_a[stream, block_of(1), at] = total.astype(BF16)
+            total = parts[block_of(0, 2), at].astype(F32) + first_a[stream, :, at].astype(F32)
+            first_a[stream, :, at] = total.astype(BF16)
 
         over(cut // STEP, one)
-        on_x = remote(first_a.at[stream, block_of(1)], second_a.at[stream], side_x)
-        on_x.start()
+        summed = first_a.at[stream]
+        away = all_to_all(summed.at[block_of(1)], far, far_peers)
+        home = all_to_all(summed.at[block_of(0)], back.at[:, part_a])
         far_x.wait_recv()
 
         def two(i):
@@ -287,18 +296,9 @@
         on_y = remote(first_b.at[stream, block_of(1)], second_b.at[stream], side_y)
         on_y.start()
         me_x.wait_recv()
-        return on_x, on_y
-
-    def finish(parts, on, sums, stream):
-        on_x, on_y = on
-        on_x.wait_recv()
-
-        def one(i):
-            at = columns(i, STEP)
-            total = parts[block_of(0), at].astype(F32) + first_a[stream, block_of(0), at].astype(F32)
-            sums[:, at] = (total + second_a[stream, :, at].astype(F32)).astype(BF16)
-
-        over(cut // STEP, one)
+        return on_y, [away, home]
+
+    def finish(parts, on_y, sums, back, stream):
         on_y.wait_recv()
 
         def two(i):
@@ -308,12 +308,13 @@
             sums[:, of] = (total + second_b[stream, :, at].astype(F32)).astype(BF16)
 
         over(rest // STEP, two)
+        return all_to_all(sums.at[:, part_b], back.at[:, part_b])
 
     swaps[2].wait_recv()
     near_out = give(part_out, [(2, downs)], 0)
 
-    grad_spread[2].wait_recv()
-    grad_spread[3].wait_recv()
+    for copy in grad_spread[1:]:
+        copy.wait_recv()
 
     def slab(which):
         return pl.ds(which * shard, shard)
@@ -351,26 +352,24 @@
         keep(1, at, hidden_grad * (gate_value * sigma))
 
     near_in = give(part_in, [(0, gates), (1, ups)], 1)
-    on_out = add_on(part_out, near_out, 0)
+    on_out, homes = add_on(part_out, near_out, back_out, far_out, 0)
     swap_gate = swap_grad(0, token_rows)
     swap_up = swap_grad(1, token_rows)
-    wait_sends(out_tokens[0])
-    finish(part_out, on_out, sent_tokens, 0)
-    home_out = all_to_all(sent_tokens, back_out)
-    on_in = add_on(part_in, near_in, 1)
+    for group in out_tokens + out_grads:
+        wait_sends(group[0])
+    homes.append(finish(part_out, on_out, sent_tokens, back_out, 0))
+    on_in, more = add_on(part_in, near_in, back_in, far_in, 1)
+    homes += more
     writes = [own_grad(2, grad_rows, swap_down, grad_down)]
-
-    wait_sends(out_grads[0])
-    finish(part_in, on_in, sent_grads, 1)
-    home_in = all_to_all(sent_grads, back_in)
+    homes.append(finish(part_in, on_in, sent_grads, back_in, 1))
     writes.append(own_grad(0, token_rows, swap_gate, grad_gate))
     writes.append(own_grad(1, token_rows, swap_up, grad_up))
-    landed(home_out)
-    landed(home_in)
+    for group in homes:
+        landed(group)
+        wait_sends(group[0])
     wait_sends(near_out + near_in)
-
-    wait_sends(swaps + list(token_spread) + list(grad_spread) + list(on_out) + list(on_in))
-    wait_sends([swap_down, swap_gate, swap_up] + home_out[0] + home_in[0])
+    wait_sends(swaps + list(token_spread) + list(grad_spread) + [on_out, on_in])
+    wait_sends([swap_down, swap_gate, swap_up])
     for copy in writes:
         copy.wait()
 
@@ -383,12 +382,14 @@
     scale_ref,
     back_out,
     back_in,
+    far_out,
+    far_in,
     *refs,
 ):
     grads, (moe_out, grad_tokens), grads_out = refs[:3], refs[3:5], refs[5:8]
-    arrived, merged, held, in_sems, out_sems = refs[8:]
+    arrived, arrived_far, merged, held, in_sems, out_sems = refs[8:]
     token_count, width = moe_out.shape
-    deep = width // (PIECES + 1)
+    cut = far_out.shape[1]
     tall = grads[0].shape[0] // PIECES
     reads, jobs = [], []
 
@@ -396,18 +397,21 @@
         copy = pltpu.make_async_copy(source, target, in_sems.at[len(reads)])
         copy.start()
         reads.append(copy)
-
-    for which, back in enumerate((back_out, back_in)):
-        for i in range(width // deep):
-            at = pl.ds(i * deep, deep)
-            read(back.at[:, at], arrived.at[which, :, at])
+        return copy
+
+    for which, back, far in ((0, back_out, far_out), (1, back_in, far_in)):
+        for i in range(width // STEP):
+            at = pl.ds(i * STEP, STEP)
+            wait = [read(back.at[:, at], arrived.at[which, :, at])]
+            if i * STEP < cut:
+                wait.append(read(far.at[:, at], arrived_far.at[which, :, at]))
             target = (moe_out, grad_tokens)[which].at[:, at]
-            jobs.append((which, i, merged.at[which, :, at], target))
+            jobs.append((wait, which, at, merged.at[which, :, at], target))
     for which, grad in enumerate(grads):
         for i in range(PIECES):
             at = pl.ds(i * tall, tall)
-            read(grad.at[at], held.at[which, at])
-            jobs.append((None, i, held.at[which, at], grads_out[which].at[at]))
+            wait = [read(grad.at[at], held.at[which, at])]
+            jobs.append((wait, None, at, held.at[which, at], grads_out[which].at[at]))
 
     named = names(flat(chosen_ref[...]), token_count)
     table = named * flat(scale_ref[...])
@@ -415,14 +419,15 @@
     fine = (table - coarse.astype(F32)).astype(BF16)
     only = named.astype(BF16)
     writes = []
-    for n, (which, i, source, target) in enumerate(jobs):
-        reads[n].wait()
+    for n, (wait, which, at, source, target) in enumerate(jobs):
+        for copy in wait:
+            copy.wait()
         if which is not None:
-            for half in range(2):
-                at = pl.ds(i * deep + half * (deep // 2), deep // 2)
-                rows = arrived[which, :, at]
-                total = dot(only, rows) if which else dot(coarse, rows) + dot(fine, rows)
-                merged[which, :, at] = total.astype(BF16)
+            total = jnp.zeros((token_count, STEP), F32)
+            for held_rows in (arrived, arrived_far)[: len(wait)]:
+                rows = held_rows[which, :, at]
+                total += dot(only, rows) if which else dot(coarse, rows) + dot(fine, rows)
+            merged[which, :, at] = total.astype(BF16)
         copy = pltpu.make_async_copy(source, target, out_sems.at[n])
         copy.start()
         writes.append(copy)
@@ -436,7 +441,7 @@
     block = n_expert * slot
     token_count, width = tokens.shape
     shard = w_down.shape[1]
-    cut = width * 3 // 5
+    cut = width // 2
     rest = width - cut
     gate_t = jnp.swapaxes(w_gate[0], 0, 1)
     up_t = jnp.swapaxes(w_up[0], 0, 1)
@@ -446,18 +451,21 @@
     weights = pltpu.VMEM((2 * shard, width), BF16)
     rows = pltpu.VMEM((4 * block, width), BF16)
     one = pltpu.VMEM((block, width), BF16)
-    copies = 3 + 4 * (n_expert - 1) + 8 + 10 + 3
+    near_copies, far_copies = n_expert - 1, n_expert
+    copies = 3 + 2 * (near_copies + far_copies + 5 + 4 + 2 * near_copies + far_copies) + 3
     results = pl.pallas_call(
         functools.partial(layer, (n_dp, n_expert, slot)),
         out_shape=[
             jax.ShapeDtypeStruct((block, width), BF16),
             jax.ShapeDtypeStruct((block, width), BF16),
+            jax.ShapeDtypeStruct((block, cut), BF16),
+            jax.ShapeDtypeStruct((block, cut), BF16),
             jax.ShapeDtypeStruct((shard, width), BF16),
             jax.ShapeDtypeStruct((shard, width), BF16),
             jax.ShapeDtypeStruct((shard, width), BF16),
         ],
         in_specs=[whole] * 7,
-        out_specs=[whole] * 5,
+        out_specs=[whole] * 7,
         scratch_shapes=[
             pltpu.VMEM((slot, n_expert), jnp.int32),
             pltpu.VMEM((slot, n_expert), F32),
@@ -472,7 +480,6 @@
             rows,
             pltpu.VMEM((2, 2 * block, cut), BF16),
             pltpu.VMEM((2, 2 * block, rest), BF16),
-            pltpu.VMEM((2, block, cut), BF16),
             pltpu.VMEM((2, block, rest), BF16),
             pltpu.VMEM((3 * shard, width), BF16),
             pltpu.VMEM((3 * shard, width), BF16),
@@ -482,7 +489,7 @@
             pltpu.VMEM((2 * shard, 4 * block), F32),
             pltpu.SemaphoreType.DMA((copies,)),
             pltpu.SemaphoreType.DMA((copies,)),
-            pltpu.SemaphoreType.DMA((14,)),
+            pltpu.SemaphoreType.DMA((16,)),
         ],
         compiler_params=pltpu.CompilerParams(
             collective_id=0, has_side_effects=True, vmem_limit_bytes=67043328
@@ -497,19 +504,21 @@
         up_t,
         w_down[0],
     )
-    moved = 2 * (PIECES + 1) + 3 * PIECES
+    stored = 2 * (width // STEP) + 3 * PIECES
+    taken = stored + 2 * (cut // STEP)
     results = pl.pallas_call(
         merge,
         out_shape=[jax.ShapeDtypeStruct((token_count, width), BF16)] * 2
         + [jax.ShapeDtypeStruct((shard, width), BF16)] * 3,
-        in_specs=[small] * 2 + [whole] * 5,
+        in_specs=[small] * 2 + [whole] * 7,
         out_specs=[whole] * 5,
         scratch_shapes=[
             pltpu.VMEM((2, block, width), BF16),
+            pltpu.VMEM((2, block, cut), BF16),
             pltpu.VMEM((2, token_count, width), BF16),
             pltpu.VMEM((3, shard, width), BF16),
-            pltpu.SemaphoreType.DMA((moved,)),
-            pltpu.SemaphoreType.DMA((moved,)),
+            pltpu.SemaphoreType.DMA((taken,)),
+            pltpu.SemaphoreType.DMA((stored,)),
         ],
         compiler_params=pltpu.CompilerParams(vmem_limit_bytes=67043328),
         name="merge",

time: 250 us -> 241 us (0.964)
  Pallas kernels: 249 us -> 241 us
    pallas_call x1, Pallas kernels: 241 us -> 230 us  [on_device(): pl.pallas_call(functools.partial(layer, (n_dp, n_expert, slot)), out_shap...]
    pallas_call x1, Pallas kernels: 8.14 us -> 10.9 us  [on_device(): pl.pallas_call(merge, out_shape=[jax.ShapeDtypeStruct((token_count, width...]
where the time goes in v4:
time: 241 us
  Pallas kernels  241 us (100%)
    pallas_call x1, Pallas kernels, on_device(): pl.pallas_call(functools.partial(layer, (n_dp, n_expert, slot)), out_shap...  230 us
    pallas_call x1, Pallas kernels, on_device(): pl.pallas_call(merge, out_shape=[jax.ShapeDtypeStruct((token_count, width...  10.9 us

profile of v4, /device:TPU:1, one launch (start us, length us, event | category | flops | bytes accessed | tf_op | source)
XLA Modules:
  0.0 241.3 jit_solution(2796719682307533689)
XLA Ops:
  0.6 229.8 %layer.1 = (bf16[128,5120]{1,0:T(8,128)(2,1)}, bf16[128,5120]{1,0:T(8,128)(2,1)}, bf16[128,2560]{1,0:T(8,128)(2,1)}, bf16[128,2560]{1,0:T(8,128)(2,1)}, bf16[192...) custom-call(s32[8,16]{1,0:T(8,128)} %bitcast.23, f32[8,16]{1,0:T(8,128)} %bitcast.25, ...), custom_call_target="tpu_custom_call" | custom-call | tf_op jit(solution)/shard_map/layer/pallas_call | solution.py:456
  230.4 10.9 %merge.1 = (bf16[256,5120]{1,0:T(8,128)(2,1)}, bf16[256,5120]{1,0:T(8,128)(2,1)}, bf16[192,5120]{1,0:T(8,128)(2,1)}, bf16[192,5120]{1,0:T(8,128)(2,1)}, bf16[192,5120]{1,0:T(8,128)(2,1)}) custom-call(s32[8,16]{1,0:T(8,128)} %bitcast.24, f32[8,16]{1,0:T(8,128)} %bitcast.26, bf16[128,5120]{1,0:T(8,128)(2,1)} %get-tuple-element.17.back_out, ...), custom_call_target="tpu_custom_call" | custom-call | tf_op jit(solution)/shard_map/merge/pallas_call | solution.py:509

commit v5 on v4

--- a/solution.py
+++ b/solution.py
@@ -375,6 +375,7 @@
 
 
 PIECES = 4
+PIECE = 1280
 
 
 def merge(
@@ -387,9 +388,9 @@
     *refs,
 ):
     grads, (moe_out, grad_tokens), grads_out = refs[:3], refs[3:5], refs[5:8]
-    arrived, arrived_far, merged, held, in_sems, out_sems = refs[8:]
+    arrived, merged, held, in_sems, out_sems = refs[8:]
     token_count, width = moe_out.shape
-    cut = far_out.shape[1]
+    block, cut = far_out.shape
     tall = grads[0].shape[0] // PIECES
     reads, jobs = [], []
 
@@ -400,34 +401,40 @@
         return copy
 
     for which, back, far in ((0, back_out, far_out), (1, back_in, far_in)):
-        for i in range(width // STEP):
-            at = pl.ds(i * STEP, STEP)
-            wait = [read(back.at[:, at], arrived.at[which, :, at])]
-            if i * STEP < cut:
-                wait.append(read(far.at[:, at], arrived_far.at[which, :, at]))
+        for i in range(width // PIECE):
+            at = pl.ds(i * PIECE, PIECE)
+            wait = [read(back.at[:, at], arrived.at[which, pl.ds(0, block), at])]
+            if i * PIECE < cut:
+                wait.append(read(far.at[:, at], arrived.at[which, pl.ds(block, block), at]))
             target = (moe_out, grad_tokens)[which].at[:, at]
-            jobs.append((wait, which, at, merged.at[which, :, at], target))
+            jobs.append((wait, which, i, merged.at[which, :, at], target))
     for which, grad in enumerate(grads):
         for i in range(PIECES):
             at = pl.ds(i * tall, tall)
             wait = [read(grad.at[at], held.at[which, at])]
-            jobs.append((wait, None, at, held.at[which, at], grads_out[which].at[at]))
+            jobs.append((wait, None, i, held.at[which, at], grads_out[which].at[at]))
 
     named = names(flat(chosen_ref[...]), token_count)
-    table = named * flat(scale_ref[...])
+    named = jnp.concatenate([named, named], axis=1)
+    scale = flat(scale_ref[...])
+    table = named * jnp.concatenate([scale, scale], axis=1)
     coarse = table.astype(BF16)
     fine = (table - coarse.astype(F32)).astype(BF16)
     only = named.astype(BF16)
     writes = []
-    for n, (wait, which, at, source, target) in enumerate(jobs):
+    for n, (wait, which, i, source, target) in enumerate(jobs):
         for copy in wait:
             copy.wait()
         if which is not None:
-            total = jnp.zeros((token_count, STEP), F32)
-            for held_rows in (arrived, arrived_far)[: len(wait)]:
-                rows = held_rows[which, :, at]
-                total += dot(only, rows) if which else dot(coarse, rows) + dot(fine, rows)
-            merged[which, :, at] = total.astype(BF16)
+            deep = len(wait) * block
+            for k in range(PIECE // 256):
+                at = pl.ds(i * PIECE + k * 256, 256)
+                rows = arrived[which, pl.ds(0, deep), at]
+                if which:
+                    total = dot(only[:, :deep], rows)
+                else:
+                    total = dot(coarse[:, :deep], rows) + dot(fine[:, :deep], rows)
+                merged[which, :, at] = total.astype(BF16)
         copy = pltpu.make_async_copy(source, target, out_sems.at[n])
         copy.start()
         writes.append(copy)
@@ -504,8 +511,8 @@
         up_t,
         w_down[0],
     )
-    stored = 2 * (width // STEP) + 3 * PIECES
-    taken = stored + 2 * (cut // STEP)
+    stored = 2 * (width // PIECE) + 3 * PIECES
+    taken = stored + 2 * (cut // PIECE)
     results = pl.pallas_call(
         merge,
         out_shape=[jax.ShapeDtypeStruct((token_count, width), BF16)] * 2
@@ -513,8 +520,7 @@
         in_specs=[small] * 2 + [whole] * 7,
         out_specs=[whole] * 5,
         scratch_shapes=[
-            pltpu.VMEM((2, block, width), BF16),
-            pltpu.VMEM((2, block, cut), BF16),
+            pltpu.VMEM((2, 2 * block, width), BF16),
             pltpu.VMEM((2, token_count, width), BF16),
             pltpu.VMEM((3, shard, width), BF16),
             pltpu.SemaphoreType.DMA((taken,)),

time: 241 us -> 239 us (level)
  Pallas kernels: 241 us -> 238 us
where the time goes in v5:
time: 239 us
  Pallas kernels  238 us (100%)
    pallas_call x1, Pallas kernels, on_device(): pl.pallas_call(functools.partial(layer, (n_dp, n_expert, slot)), out_shap...  230 us
    pallas_call x1, Pallas kernels, on_device(): pl.pallas_call(merge, out_shape=[jax.ShapeDtypeStruct((token_count, width...  8.5 us

profile of v5, /device:TPU:1, one launch (start us, length us, event | category | flops | bytes accessed | tf_op | source)
XLA Modules:
  0.0 239.0 jit_solution(4208080708077694579)
XLA Ops:
  0.6 229.8 %layer.1 = (bf16[128,5120]{1,0:T(8,128)(2,1)}, bf16[128,5120]{1,0:T(8,128)(2,1)}, bf16[128,2560]{1,0:T(8,128)(2,1)}, bf16[128,2560]{1,0:T(8,128)(2,1)}, bf16[192...) custom-call(s32[8,16]{1,0:T(8,128)} %bitcast.23, f32[8,16]{1,0:T(8,128)} %bitcast.25, ...), custom_call_target="tpu_custom_call" | custom-call | tf_op jit(solution)/shard_map/layer/pallas_call | solution.py:463
  230.4 8.5 %merge.1 = (bf16[256,5120]{1,0:T(8,128)(2,1)}, bf16[256,5120]{1,0:T(8,128)(2,1)}, bf16[192,5120]{1,0:T(8,128)(2,1)}, bf16[192,5120]{1,0:T(8,128)(2,1)}, bf16[192,5120]{1,0:T(8,128)(2,1)}) custom-call(s32[8,16]{1,0:T(8,128)} %bitcast.24, f32[8,16]{1,0:T(8,128)} %bitcast.26, bf16[128,5120]{1,0:T(8,128)(2,1)} %get-tuple-element.17.back_out, ...), custom_call_target="tpu_custom_call" | custom-call | tf_op jit(solution)/shard_map/merge/pallas_call | solution.py:516
